TPU v7x, 256 devices: a whole 4x4x8 slice. The times are simulated.
256 devices in a mesh: hier: 8 (over z), row: 32 (over x, y, core).
Axes of the slice: x: 4, y: 4, z: 8, core: 2. Of those that a mesh axis runs over, the one named last changes fastest.
Arguments:
- density: float32 [2, 16, 512, 512], P(None, 'hier', 'row')
- hamiltonian: float32 [512, 512], P('row')
- couplings: float32 [8, 512], replicated, may hold values from -5 to 5
- decay_rates: float32 [8], replicated, may hold values from 0.1 to 1
- bath_coeffs: float32 [2, 8], replicated, may hold values from 0.3 to 1.2
- levels: int32 [16, 8], replicated, may hold values from 0 to 2, as said below
- neighbours: int32 [2, 16, 8], replicated, may hold values from -1 to 15, as said below
Outputs:
- evolved: float32 [2, 16, 512, 512], P(None, 'hier', 'row')
Inputs may be any that keep to these rules, and one draw needn't show every extreme that they name: levels[m, k] counts the excitations of mode k in matrix m; the kept set holds the vector of zeros, then unit vectors, then vectors of total two, stored in an order drawn from the seed. neighbours[0, m, k] is the index of the kept matrix whose levels are those of m plus one in mode k, neighbours[1, m, k] the one with one less, -1 where that matrix is not kept.
All inputs are finite; a program needn't handle non-finite values.
Results may differ from a plain program's by a relative error of at most 0.0001.
Values sent between devices are 32-bit elements; how exact they have to be, the bound alone decides.
No kernel may reach another device: no remote copies, remote signals or barrier semaphores. Data moves between devices by JAX's collectives and lax.ppermute only.
A program may use at most 64 MiB of HBM per device.

v0:
```python
import jax
import jax.numpy as jnp
from jax import lax
from jax.experimental import pallas as pl
from jax.experimental.pallas import tpu as pltpu
from jax.sharding import PartitionSpec as P

time_step = 0.25
A1 = time_step
A2 = A1 * time_step / 2
A3 = A2 * time_step / 3

PLANES = 8
ROWS = 32
EDGES = 264


VMEM = pl.BlockSpec(memory_space=pltpu.VMEM)
ANY = pl.BlockSpec(memory_space=pl.ANY)
SMEM = pl.BlockSpec(memory_space=pltpu.SMEM)
PARAMS = pltpu.CompilerParams(vmem_limit_bytes=24 << 20)


def f32(*shape):
    return pltpu.VMEM(shape, jnp.float32)


def near(*arrays):
    return [pltpu.with_memory_space_constraint(array, pltpu.VMEM) for array in arrays]


def my_plane():
    return lax.axis_index("hier").astype(jnp.int32)


def split_kernel(density, hamiltonian, copies, near_blocks, far_blocks, rows, own, tiles, sems):
    plane = my_plane()
    group = lax.axis_index("row").astype(jnp.int32)
    fetch = pltpu.make_async_copy(density, rows, sems.at[0])
    fetch_own = pltpu.make_async_copy(hamiltonian, own, sems.at[1])
    fetch.start()
    fetch_own.start()
    fetch.wait()
    for p in range(4):
        for j in range(4):
            tiles[pl.ds(64 * p + 16 * j, 16), :] = rows[p, :, 128 * j : 128 * j + 128]
    for s in range(PLANES):
        first = 2 * (plane ^ s)
        target = far_blocks if s & 4 else near_blocks
        for a in range(2):
            picked = tiles[pl.ds(first + a, 16, stride=16), :]
            for p in range(4):
                target[s & 3, 8 * p + 4 * a : 8 * p + 4 * a + 4, :] = picked[4 * p : 4 * p + 4]
    fetch_own.wait()
    turned = pltpu.roll(own[...], (512 - 16 * group) & 511, 1)
    lane = lax.broadcasted_iota(jnp.int32, (16, 128), 1)
    main = jnp.where(lane < 16, 0.5 * turned[:, :128], turned[:, :128])
    last = 0.5 * turned[:, 256:384]
    lane = lax.broadcasted_iota(jnp.int32, (8, 128), 1)
    last = jnp.where(lane < 16, last[:8], pltpu.roll(last[8:], 16, 1))
    block = jnp.concatenate([main, turned[:, 128:256], last], axis=0)
    for r in range(ROWS):
        copies[r] = block


def join_symmetric(blocks, upper):
    lane = lax.broadcasted_iota(jnp.int32, (8, 128), 1)
    for r in range(ROWS):
        tile, offset = r // 8, 16 * (r % 8)
        for half in range(2):
            at = 8 * half
            first = blocks[r, at : at + 8, :]
            second = blocks[r, 16 + at : 24 + at, :]
            last = blocks[r, 32:40, :]
            if offset:
                first = pltpu.roll(first, offset, 1)
                second = pltpu.roll(second, offset, 1)
            if (offset - 16 * half) % 128:
                last = pltpu.roll(last, (offset - 16 * half) % 128, 1)
            last = jnp.where((lane >= offset) & (lane < offset + 16), last, 0.0)
            if offset:
                parts = [
                    jnp.where(lane >= offset, first, 0.0),
                    jnp.where(lane < offset, first, second),
                    jnp.where(lane < offset, second, last),
                ]
            else:
                parts = [first, second, last]
            parts.append(jnp.zeros_like(first))
            for i in range(4):
                col = 128 * ((tile + i) % 4)
                upper[16 * r + at : 16 * r + at + 8, col : col + 128] = parts[i]
    value = upper[...]
    return value + jnp.transpose(value)


def pack_kernel(near_blocks, far_blocks, *out):
    for s in range(1, 4):
        out[s - 1][0] = near_blocks[s]
        out[s - 1][1] = far_blocks[s]


def prepare(levels, neighbours, decay, bath, couplings, codes, ints, floats, fields):
    plane = my_plane()
    row = 16 * lax.axis_index("row").astype(jnp.int32) + 2 * plane

    def place(g):
        return (plane ^ (g >> 1)) * 4 + (g & 1)

    count = 0
    for m in range(16):
        for k in range(8):
            lower = neighbours[1, k, m]
            codes[count] = lower * 128 + (8 * m + k)
            count = count + (lower >= 0).astype(jnp.int32)
    ints[3, 0] = count

    def unpack(e, carry):
        code = codes[e]
        m = (code >> 3) & 15
        k = code & 7
        level = levels[k, m].astype(jnp.float32)
        ints[0, e] = place(m)
        ints[1, e] = place(code >> 7)
        ints[2, e] = 8 * k
        floats[0, e] = level * bath[1, k]
        floats[1, e] = level * bath[0, k]
        return carry

    lax.fori_loop(0, count, unpack, 0)
    for m in range(16):
        total = levels[0, m].astype(jnp.float32) * decay[0]
        for k in range(1, 8):
            total = total + levels[k, m].astype(jnp.float32) * decay[k]
        floats[2, place(m)] = total

    values = couplings[...]
    lane = lax.broadcasted_iota(jnp.int32, values.shape, 1)
    for a in range(2):
        own = jnp.sum(jnp.where(lane == row + a, values, 0.0), axis=1, keepdims=True)
        own = jnp.broadcast_to(own, (8, 128))
        for j in range(4):
            here = pl.ds(4 * a + j, 8, stride=8)
            there = values[:, 128 * j : 128 * j + 128]
            fields[0, here, :] = own - there
            fields[1, here, :] = own + there
            fields[2, here, :] = there


def mix(ints, floats, fields, source, both, right):
    def step(e, carry):
        m = ints[0, e]
        q = ints[1, e]
        k = pl.multiple_of(ints[2, e], 8)
        even = floats[0, e]
        odd = floats[1, e]
        xm, ym = source[m], source[m + 2]
        xq, yq = source[q], source[q + 2]
        if both is not None:
            d = fields[0, pl.ds(k, 8), :]
            f = odd * d
            g = even * fields[1, pl.ds(k, 8), :]
            both[m] = both[m] + (g * xq + f * yq)
            both[m + 2] = both[m + 2] + (g * yq - f * xq)
            both[q] = both[q] + d * ym
            both[q + 2] = both[q + 2] - d * xm
        if right is not None:
            c = fields[2, pl.ds(k, 8), :]
            g = even * c
            f = odd * c
            right[m] = right[m] + (g * xq - f * yq)
            right[m + 2] = right[m + 2] + (g * yq + f * xq)
            right[q] = right[q] - c * ym
            right[q + 2] = right[q + 2] + c * xm
        return carry

    lax.fori_loop(0, ints[3, 0], step, 0)


def decayed(floats, source):
    parts = []
    for s in range(PLANES):
        for part in range(2):
            for m in range(2):
                parts.append((-floats[2, 4 * s + m]) * source[4 * s + 2 * part + m])
    return jnp.stack(parts)


def gather_rows(ref):
    return jnp.concatenate(
        [
            jnp.concatenate([ref[pl.ds(4 * a + j, 32, stride=8), :] for j in range(4)], axis=1)
            for a in range(2)
        ],
        axis=0,
    )


def spread_rows(ref, value):
    for a in range(2):
        for j in range(4):
            ref[pl.ds(4 * a + j, 32, stride=8), :] = value[
                32 * a : 32 * a + 32, 128 * j : 128 * j + 128
            ]


def halves(value):
    high = value.astype(jnp.bfloat16)
    low = (value - high.astype(jnp.float32)).astype(jnp.bfloat16)
    return high, low


def times_i(value):
    value = value.reshape(PLANES, 2, 2, 8, 128)
    return jnp.concatenate([-value[:, 1:], value[:, :1]], axis=1).reshape(32, 8, 128)


def swap_blocks(value):
    lead = value.shape[0]
    block = lax.broadcasted_iota(jnp.int32, (8, 128), 1) // 16
    for k in range(3):
        width = 16 << k
        low = ((block >> k) & 1) == 0
        pairs = value.reshape(lead, 4 >> k, 2, 1 << k, 8, 128)
        zero, one = pairs[:, :, 0], pairs[:, :, 1]
        shape = zero.shape
        zero = zero.reshape(-1, 128)
        one = one.reshape(-1, 128)
        up = pltpu.roll(one, width, 1)
        down = pltpu.roll(zero, 128 - width, 1)
        low = jnp.broadcast_to(low[None], (zero.shape[0] // 8, 8, 128)).reshape(-1, 128)
        new_zero = jnp.where(low, zero, up).reshape(shape)
        new_one = jnp.where(low, down, one).reshape(shape)
        value = jnp.stack([new_zero, new_one], axis=2).reshape(lead, 8, 8, 128)
    return value


def rows_kernel(levels, neighbours, decay, bath, couplings, h, *refs):
    near_blocks, far_blocks, *pairs, message, h_high, h_low = refs[:8]
    codes, ints, floats, fields, state, first, right, second, rows, p, ep, bp, upper = refs[8:]
    plane = my_plane()
    prepare(levels, neighbours, decay, bath, couplings, codes, ints, floats, fields)
    high, low = halves(join_symmetric(h, upper))
    h_high[...] = high
    h_low[...] = low

    state[0:4] = near_blocks[0].reshape(4, 8, 128)
    state[16:20] = far_blocks[0].reshape(4, 8, 128)
    for s in range(1, 4):
        state[4 * s : 4 * s + 4] = pairs[s - 1][0].reshape(4, 8, 128)
        state[4 * s + 16 : 4 * s + 20] = pairs[s - 1][1].reshape(4, 8, 128)
    first[...] = decayed(floats, state)
    right[...] = jnp.zeros_like(right)
    mix(ints, floats, fields, state, first, right)
    first[...] = A2 * state[...] + A3 * first[...]
    second[...] = decayed(floats, first)
    mix(ints, floats, fields, first, second, None)

    def product(value):
        count = value.shape[0]
        value_high, value_low = halves(value)
        main = jnp.dot(
            jnp.concatenate([value_high, value_low], axis=0),
            high,
            preferred_element_type=jnp.float32,
        )
        rest = jnp.dot(value_high, low, preferred_element_type=jnp.float32)
        return main[:count] + main[count:] + rest

    def apply(values):
        stacked = []
        for value in values:
            rows[...] = value.reshape(256, 128)
            stacked.append(gather_rows(rows))
        result = product(jnp.concatenate(stacked, axis=0))
        out = []
        for i in range(len(values)):
            spread_rows(rows, result[64 * i : 64 * i + 64])
            out.append(times_i(rows[...].reshape(32, 8, 128)))
        return out

    s_value = state[...]
    (p_value,) = apply([s_value])
    p[...] = p_value
    v1, edge = apply([first[...] + A3 * p_value, p_value + right[...]])
    damped = decayed(floats, p)
    ep[...] = damped
    bp[...] = damped + edge
    mix(ints, floats, fields, p, ep, bp)
    k_value = A2 * p_value + 3 * A3 * bp[...]
    z_value = 0.5 * A1 * s_value + v1 + A3 * ep[...] + 0.5 * second[...]
    v2 = z_value + 0.5 * A1 * s_value + 0.5 * second[...]
    (g_value,) = apply([v2])
    p[...] = z_value
    ep[...] = g_value + decayed(floats, p)
    mix(ints, floats, fields, p, ep, None)
    both = jnp.concatenate(
        [k_value.reshape(8, 4, 8, 128), ep[...].reshape(8, 4, 8, 128)], axis=1
    )
    both = swap_blocks(both)
    for s in range(PLANES):
        start = 2 * (plane ^ s)
        for b in range(8):
            for a in range(2):
                message[pl.ds(start + 16 * b + a, 4, stride=128), :] = both[
                    s, b, 4 * a : 4 * a + 4, :
                ]


def columns_kernel(received, h_high, h_low, message, total):
    value = received[...]
    high, low = halves(value)
    main = jnp.dot(
        h_high[...], jnp.concatenate([high, low], axis=1), preferred_element_type=jnp.float32
    )
    rest = jnp.dot(h_low[...], high, preferred_element_type=jnp.float32)
    z = main[:, :128] + main[:, 128:] + rest
    lane = lax.broadcasted_iota(jnp.int32, z.shape, 1)
    other = pltpu.roll(value, 64, 1)
    result = jnp.where(
        lane < 32, pltpu.roll(z, 96, 1) + other, pltpu.roll(z, 32, 1) - other
    )
    total[...] = result
    tiles = result.reshape(32, 2, 8, 128)
    upper = pltpu.roll(tiles[:, 1].reshape(256, 128), 64, 1)
    lane = lax.broadcasted_iota(jnp.int32, upper.shape, 1)
    message[...] = jnp.where(lane < 64, tiles[:, 0].reshape(256, 128), upper)


def base_kernel(density, total, base):
    base[...] = density[...] + jnp.transpose(total[...])[:64]


def finish_kernel(base, received, out):
    value = swap_blocks(received[...].reshape(4, 8, 8, 128))
    for g in range(4):
        for half in range(2):
            for p in range(4):
                row = slice(16 * p + 8 * half, 16 * p + 8 * half + 8)
                col = slice(128 * g, 128 * g + 128)
                part = value[g, 4 * half + p]
                out[row, col] = base[row, col] + part if p < 2 else base[row, col] - part


def on_device(density, hamiltonian, couplings, decay_rates, bath_coeffs, levels, neighbours):
    copies, near_blocks, far_blocks = pl.pallas_call(
        split_kernel,
        out_shape=[f32(ROWS, 40, 128), f32(4, 32, 128), f32(4, 32, 128)],
        in_specs=[ANY] * 2,
        out_specs=[VMEM] * 3,
        scratch_shapes=[
            pltpu.VMEM((4, 16, 512), jnp.float32),
            pltpu.VMEM((16, 512), jnp.float32),
            pltpu.VMEM((256, 128), jnp.float32),
            pltpu.SemaphoreType.DMA((2,)),
        ],
        name="split",
        compiler_params=PARAMS,
    )(density.reshape(4, 16, 512), hamiltonian)
    blocks = lax.all_to_all(copies, "row", 0, 0, tiled=True)

    def swap(block, s):
        return lax.ppermute(block, "hier", [(i, i ^ s) for i in range(PLANES)])

    far_blocks = swap(far_blocks, 4)
    packed = pl.pallas_call(
        pack_kernel,
        out_shape=[f32(2, 32, 128)] * 3,
        in_specs=[VMEM] * 2,
        out_specs=[VMEM] * 3,
        name="pack",
        compiler_params=PARAMS,
    )(*near(near_blocks, far_blocks))
    pairs = [swap(packed[s - 1], s) for s in (1, 2, 3)]

    bf16 = pltpu.VMEM((512, 512), jnp.bfloat16)
    whole = pltpu.VMEM((32, 8, 128), jnp.float32)
    message, h_high, h_low = pl.pallas_call(
        rows_kernel,
        out_shape=[f32(512, 128), bf16, bf16],
        in_specs=[SMEM] * 4 + [VMEM] * 7,
        out_specs=[VMEM] * 3,
        scratch_shapes=[
            pltpu.SMEM((EDGES,), jnp.int32),
            pltpu.SMEM((4, EDGES), jnp.int32),
            pltpu.SMEM((3, EDGES), jnp.float32),
            pltpu.VMEM((3, 64, 128), jnp.float32),
            *[whole] * 4,
            pltpu.VMEM((256, 128), jnp.float32),
            *[whole] * 3,
            pltpu.VMEM((512, 512), jnp.float32),
        ],
        name="rows",
        compiler_params=PARAMS,
    )(
        levels.T,
        jnp.swapaxes(neighbours, 1, 2),
        decay_rates,
        bath_coeffs,
        couplings,
        *near(blocks, near_blocks, far_blocks, *pairs),
    )

    received = lax.all_to_all(
        message.reshape(256, 2, 128), ("row", "hier"), 0, 0, tiled=True
    ).reshape(512, 128)

    message, total = pl.pallas_call(
        columns_kernel,
        out_shape=[f32(256, 128), f32(512, 128)],
        in_specs=[VMEM] * 3,
        out_specs=[VMEM] * 2,
        name="columns",
        compiler_params=PARAMS,
    )(*near(received, h_high, h_low))

    received = lax.all_to_all(
        message.reshape(ROWS, 8, 128), "row", 0, 0, tiled=True
    ).reshape(256, 128)

    base = pl.pallas_call(
        base_kernel, out_shape=f32(64, 512), in_specs=[VMEM] * 2, out_specs=VMEM, name="base",
        compiler_params=PARAMS,
    )(density.reshape(64, 512), *near(total))
    out = pl.pallas_call(
        finish_kernel,
        out_shape=jax.ShapeDtypeStruct((64, 512), jnp.float32),
        in_specs=[VMEM] * 2,
        out_specs=VMEM,
        name="finish",
        compiler_params=PARAMS,
    )(*near(base, received))
    return out.reshape(2, 2, 16, 512)


def solution(mesh):
    in_specs = (P(None, "hier", "row", None), P("row", None), P(), P(), P(), P(), P())
    out_specs = P(None, "hier", "row", None)
    return jax.shard_map(
        on_device, mesh=mesh, in_specs=in_specs, out_specs=out_specs, check_vma=False
    )
```

profile of v0, /device:TPU:1, one launch (start us, length us, event | category | flops | bytes accessed | tf_op | source)
XLA Modules:
  0.0 78.0 jit_solution(14665897076857784677)
XLA Ops:
  0.0 0.0 copy-start
  0.0 0.9 %copy-done = f32[2,2,16,512]{3,2,1,0:T(8,128)S(1)} copy-done((f32[2,2,16,512]{3,2,1,0:T(8,128)S(1)}, f32[2,2,16,512]{3,2,1,0:T(8,128)}, u32[]{:S(2)}) %copy-start) | copy-done | bytes 131096
  0.9 0.0 copy-start.2
  0.9 0.8 copy-done.2
  1.7 1.3 %split.1 = (f32[32,40,128]{2,1,0:T(8,128)}, f32[4,32,128]{2,1,0:T(8,128)S(1)}, f32[4,32,128]{2,1,0:T(8,128)S(1)}) custom-call(f32[4,16,512]{2,1,0:T(8,128)S(1)} %bitcast.11, f32[16,512]{1,0:T(8,128)S(1)} %copy-done.2), custom_call_target="tpu_custom_call" | custom-call | tf_op jit(solution)/shard_map/split/pallas_call | solution.py:346
  2.9 8.6 %all-to-all-start = ((f32[32,40,128]{2,1,0:T(8,128)}), f32[32,40,128]{2,1,0:T(8,128)S(1)}, u32[]{:S(2)}, u32[]{:S(2)}) async-start(f32[32,40,128]{2,1,0:T(8,128)} %get-tuple-element.16), calls=%async_computation | async-start | bytes 1310720 | tf_op jit(solution)/shard_map/all_to_all | solution.py:360
  11.5 7.0 %collective-permute-start = (f32[4,32,128]{2,1,0:T(8,128)S(1)}, f32[4,32,128]{2,1,0:T(8,128)S(1)}, u32[]{:S(2)}, u32[]{:S(2)}) collective-permute-start(f32[4,32,128]{2,1,0:T(8,128)S(1)} %get-tuple-element.18), channel_id=1, source_target_pairs={{0,128},{32,160},{64,192},{96,224},{128,0},{160,32},{192,64},{224,... | collective-permute-start | bytes 196616 | tf_op jit(solution)/shard_map/ppermute | solution.py:363
  18.5 2.2 %collective-permute-done.far_blocks.refs_1_ = f32[4,32,128]{2,1,0:T(8,128)S(1)} collective-permute-done((f32[4,32,128]{2,1,0:T(8,128)S(1)}, f32[4,32,128]{2,1,0:T(8,128)S(1)}, u32[]{:S(2)}, u32[]{:S(2)}) %collective-permute-start) | collective-permute-done | bytes 65568 | tf_op jit(solution)/shard_map/ppermute | solution.py:363
  20.8 0.0 copy-start.3
  20.8 0.0 copy-start.5
  20.8 0.0 copy-start.7
  20.8 0.0 copy-start.4
  20.8 0.8 %collective-permute-start.1 = (f32[2,32,128]{2,1,0:T(8,128)S(1)}, f32[2,32,128]{2,1,0:T(8,128)S(1)}, u32[]{:S(2)}, u32[]{:S(2)}) collective-permute-start(f32[2,32,128]{2,1,0:T(8,128)S(1)} %get-tuple-element.19), channel_id=1, source_target_pairs={{0,32},{32,0},{64,96},{96,64},{128,160},{160,128},{192,224},{224,1... | collective-permute-start | bytes 98312 | tf_op jit(solution)/shard_map/ppermute | solution.py:363
  21.6 2.1 %collective-permute-start.2 = (f32[2,32,128]{2,1,0:T(8,128)S(1)}, f32[2,32,128]{2,1,0:T(8,128)S(1)}, u32[]{:S(2)}, u32[]{:S(2)}) collective-permute-start(f32[2,32,128]{2,1,0:T(8,128)S(1)} %get-tuple-element.20), channel_id=1, source_target_pairs={{0,64},{32,96},{64,0},{96,32},{128,192},{160,224},{192,128},{224,1... | collective-permute-start | bytes 98312 | tf_op jit(solution)/shard_map/ppermute | solution.py:363
  23.7 0.7 collective-permute-start.3
  24.4 0.0 collective-permute-done.1.refs_2_
  24.4 0.9 %collective-permute-done.2.refs_3_ = f32[2,32,128]{2,1,0:T(8,128)S(1)} collective-permute-done((f32[2,32,128]{2,1,0:T(8,128)S(1)}, f32[2,32,128]{2,1,0:T(8,128)S(1)}, u32[]{:S(2)}, u32[]{:S(2)}) %collective-permute-start.2) | collective-permute-done | bytes 32800 | tf_op jit(solution)/shard_map/ppermute | solution.py:363
  25.4 3.0 %collective-permute-done.3.refs_4_ = f32[2,32,128]{2,1,0:T(8,128)S(1)} collective-permute-done((f32[2,32,128]{2,1,0:T(8,128)S(1)}, f32[2,32,128]{2,1,0:T(8,128)S(1)}, u32[]{:S(2)}, u32[]{:S(2)}) %collective-permute-start.3) | collective-permute-done | bytes 32800 | tf_op jit(solution)/shard_map/ppermute | solution.py:363
  28.3 0.0 all-to-all-done.h
  28.3 0.0 copy-start.6
  28.3 0.0 copy-done.3
  28.3 0.0 copy-done.5
  28.3 0.0 copy-done.7
  28.4 0.0 copy-done.4
  28.4 0.6 copy-done.6
  29.0 4.8 %rows.1 = (f32[512,128]{1,0:T(8,128)S(1)}, bf16[512,512]{1,0:T(8,128)(2,1)S(1)}, bf16[512,512]{1,0:T(8,128)(2,1)S(1)}) custom-call(s32[8,16]{1,0:T(8,128)S(1)} %bitcast.15, s32[2,8,16]{2,1,0:T(8,128)S(1)} %bitcast.14, f32[8]{0:T(128)S(1)} %copy-done.7, f32[2,8]{1,0:T(2,128)S(1)} %copy-done.6, f32[8,512]{1,0:T(8,128)S(1)} %copy-done.3, ...), custom_call_target="tpu_custom_call" | custom-call | tf_op jit(solution)/shard_map/rows/pallas_call | solution.py:378
  33.8 29.9 %all_to_all.15 = f32[256,2,128]{2,1,0:T(2,128)S(1)} all-to-all(f32[256,2,128]{2,1,0:T(2,128)S(1)} %bitcast.13), channel_id=1, replica_groups=mesh['hier'=8,'row'=32] {'row','hier'}, dimensions={0} | all-to-all | bytes 524288 | tf_op jit(solution)/shard_map/all_to_all | solution.py:404
  63.7 1.2 %columns.1 = (f32[256,128]{1,0:T(8,128)}, f32[512,128]{1,0:T(8,128)S(1)}) custom-call(f32[512,128]{1,0:T(8,128)S(1)} %bitcast.9, bf16[512,512]{1,0:T(8,128)(2,1)S(1)} %get-tuple-element.23.h_high, bf16[512,512]{1,0:T(8,128)(2,1)S(1)} %get-tuple-element.24.h_low), custom_call_target="tpu_custom_call" | custom-call | tf_op jit(solution)/shard_map/columns/pallas_call | solution.py:408
  65.0 0.0 copy-start.1
  65.0 4.4 %all-to-all-start.2 = ((f32[32,8,128]{2,1,0:T(8,128)}), f32[32,8,128]{2,1,0:T(8,128)S(1)}, u32[]{:S(2)}, u32[]{:S(2)}) async-start(f32[32,8,128]{2,1,0:T(8,128)} %bitcast.6), calls=%async_computation.2 | async-start | bytes 262144 | tf_op jit(solution)/shard_map/all_to_all | solution.py:417
  69.3 0.0 copy-done.1
  69.3 0.1 base.1
  69.5 7.7 %all-to-all-done.2 = f32[32,8,128]{2,1,0:T(8,128)S(1)} async-done(((f32[32,8,128]{2,1,0:T(8,128)}), f32[32,8,128]{2,1,0:T(8,128)S(1)}, u32[]{:S(2)}, u32[]{:S(2)}) %all-to-all-start.2) | async-done | bytes 131104 | tf_op jit(solution)/shard_map/all_to_all | solution.py:417
  77.1 0.9 %finish.1 = f32[64,512]{1,0:T(8,128)} custom-call(f32[64,512]{1,0:T(8,128)S(1)} %base.1, f32[256,128]{1,0:T(8,128)S(1)} %bitcast.10), custom_call_target="tpu_custom_call" | custom-call | tf_op jit(solution)/shard_map/finish/pallas_call | solution.py:425
  (1 shorter events, 0.0 us)
Async XLA Ops:
  0.0 0.9 %copy-start = (f32[2,2,16,512]{3,2,1,0:T(8,128)S(1)}, f32[2,2,16,512]{3,2,1,0:T(8,128)}, u32[]{:S(2)}) copy-start(f32[2,2,16,512]{3,2,1,0:T(8,128)} %param.7) | copy-start | bytes 393220
  0.9 0.8 copy-start.2
  2.9 25.4 %all-to-all-start = ((f32[32,40,128]{2,1,0:T(8,128)}), f32[32,40,128]{2,1,0:T(8,128)S(1)}, u32[]{:S(2)}, u32[]{:S(2)}) async-start(f32[32,40,128]{2,1,0:T(8,128)} %get-tuple-element.16), calls=%async_computation | async-start | bytes 1310720 | tf_op jit(solution)/shard_map/all_to_all | solution.py:360
  11.5 9.2 %collective-permute-start = (f32[4,32,128]{2,1,0:T(8,128)S(1)}, f32[4,32,128]{2,1,0:T(8,128)S(1)}, u32[]{:S(2)}, u32[]{:S(2)}) collective-permute-start(f32[4,32,128]{2,1,0:T(8,128)S(1)} %get-tuple-element.18), channel_id=1, source_target_pairs={{0,128},{32,160},{64,192},{96,224},{128,0},{160,32},{192,64},{224,... | collective-permute-start | bytes 196616 | tf_op jit(solution)/shard_map/ppermute | solution.py:363
  20.8 7.6 %copy-start.3 = (f32[8,512]{1,0:T(8,128)S(1)}, f32[8,512]{1,0:T(8,128)}, u32[]{:S(2)}) copy-start(f32[8,512]{1,0:T(8,128)} %couplings.1) | copy-start | bytes 49156
  20.8 7.6 %copy-start.5 = (s32[16,8]{0,1:T(8,128)S(1)}, s32[16,8]{0,1:T(8,128)}, u32[]{:S(2)}) copy-start(s32[16,8]{0,1:T(8,128)} %param.12) | copy-start | bytes 1540
  20.8 7.6 %copy-start.7 = (f32[8]{0:T(128)S(1)}, f32[8]{0:T(128)}, u32[]{:S(2)}) copy-start(f32[8]{0:T(128)} %decay.1) | copy-start | bytes 100
  20.8 7.6 %copy-start.4 = (s32[2,16,8]{1,2,0:T(8,128)S(1)}, s32[2,16,8]{1,2,0:T(8,128)}, u32[]{:S(2)}) copy-start(s32[2,16,8]{1,2,0:T(8,128)} %param.13) | copy-start | bytes 3076
  20.8 3.6 %collective-permute-start.1 = (f32[2,32,128]{2,1,0:T(8,128)S(1)}, f32[2,32,128]{2,1,0:T(8,128)S(1)}, u32[]{:S(2)}, u32[]{:S(2)}) collective-permute-start(f32[2,32,128]{2,1,0:T(8,128)S(1)} %get-tuple-element.19), channel_id=1, source_target_pairs={{0,32},{32,0},{64,96},{96,64},{128,160},{160,128},{192,224},{224,1... | collective-permute-start | bytes 98312 | tf_op jit(solution)/shard_map/ppermute | solution.py:363
  21.6 3.8 %collective-permute-start.2 = (f32[2,32,128]{2,1,0:T(8,128)S(1)}, f32[2,32,128]{2,1,0:T(8,128)S(1)}, u32[]{:S(2)}, u32[]{:S(2)}) collective-permute-start(f32[2,32,128]{2,1,0:T(8,128)S(1)} %get-tuple-element.20), channel_id=1, source_target_pairs={{0,64},{32,96},{64,0},{96,32},{128,192},{160,224},{192,128},{224,1... | collective-permute-start | bytes 98312 | tf_op jit(solution)/shard_map/ppermute | solution.py:363
  23.7 4.6 %collective-permute-start.3 = (f32[2,32,128]{2,1,0:T(8,128)S(1)}, f32[2,32,128]{2,1,0:T(8,128)S(1)}, u32[]{:S(2)}, u32[]{:S(2)}) collective-permute-start(f32[2,32,128]{2,1,0:T(8,128)S(1)} %get-tuple-element.21), channel_id=1, source_target_pairs={{0,96},{32,64},{64,32},{96,0},{128,224},{160,192},{192,160},{224,1... | collective-permute-start | bytes 98312 | tf_op jit(solution)/shard_map/ppermute | solution.py:363
  28.3 0.7 copy-start.6
  65.0 4.4 %copy-start.1 = (f32[2,2,16,512]{3,2,1,0:T(8,128)S(1)}, f32[2,2,16,512]{3,2,1,0:T(8,128)}, u32[]{:S(2)}) copy-start(f32[2,2,16,512]{3,2,1,0:T(8,128)} %param.7) | copy-start | bytes 393220
  65.0 12.2 %all-to-all-start.2 = ((f32[32,8,128]{2,1,0:T(8,128)}), f32[32,8,128]{2,1,0:T(8,128)S(1)}, u32[]{:S(2)}, u32[]{:S(2)}) async-start(f32[32,8,128]{2,1,0:T(8,128)} %bitcast.6), calls=%async_computation.2 | async-start | bytes 262144 | tf_op jit(solution)/shard_map/all_to_all | solution.py:417
where the time goes:
time: 78.4 us; the launch traced here: 78 us
  blocking collectives  29.9 us (38%)
  starting transfers between devices  23.6 us (30%)
  waiting for transfers between devices  13.8 us (18%)
  Pallas kernels  8.36 us (11%)
  local copies, waits for them, and re-layouts  2.33 us (3%)
    all_to_all x1, blocking collectives, on_device(): lax.all_to_all(message.reshape(256, 2, 128), ('row', 'hier'), 0, 0, tiled...  29.9 us
    ppermute x4, starting transfers between devices, swap(): return lax.ppermute(block, 'hier', [(i, i ^ s) for i in range(PLANES)])  10.6 us
    all_to_all x1, starting transfers between devices, on_device(): blocks = lax.all_to_all(copies, 'row', 0, 0, tiled=True)  8.59 us
    all_to_all x1, waiting for transfers between devices, on_device(): lax.all_to_all(message.reshape(ROWS, 8, 128), 'row', 0, 0, tiled=True)  7.65 us
    ppermute x4, waiting for transfers between devices, swap(): return lax.ppermute(block, 'hier', [(i, i ^ s) for i in range(PLANES)])  6.14 us
    pallas_call x1, Pallas kernels, on_device(): pl.pallas_call(rows_kernel, out_shape=[f32(512, 128), bf16, bf16], in_spe...  4.81 us
    all_to_all x1, starting transfers between devices, on_device(): lax.all_to_all(message.reshape(ROWS, 8, 128), 'row', 0, 0, tiled=True)  4.36 us
    unnamed x16, local copies, waits for them, and re-layouts  2.33 us
  transfers between devices with their start and end apart: 6, of which 4 were waited for; matrix products, arithmetic and copies ran while one was open for 0% of the time, Pallas kernels for 0%

commit v1 on v0

--- a/solution.py
+++ b/solution.py
@@ -17,6 +17,7 @@
 
 VMEM = pl.BlockSpec(memory_space=pltpu.VMEM)
 ANY = pl.BlockSpec(memory_space=pl.ANY)
+HBM = pl.BlockSpec(memory_space=pltpu.HBM)
 SMEM = pl.BlockSpec(memory_space=pltpu.SMEM)
 PARAMS = pltpu.CompilerParams(vmem_limit_bytes=24 << 20)
 
@@ -29,17 +30,33 @@
     return [pltpu.with_memory_space_constraint(array, pltpu.VMEM) for array in arrays]
 
 
+def far(*arrays):
+    return [pltpu.with_memory_space_constraint(array, pltpu.HBM) for array in arrays]
+
+
 def my_plane():
     return lax.axis_index("hier").astype(jnp.int32)
 
 
-def split_kernel(density, hamiltonian, copies, near_blocks, far_blocks, rows, own, tiles, sems):
+def split_kernel(density, hamiltonian, copies, near_blocks, far_blocks, *scratch):
+    rows, own, block, tiles, sems = scratch
     plane = my_plane()
     group = lax.axis_index("row").astype(jnp.int32)
-    fetch = pltpu.make_async_copy(density, rows, sems.at[0])
-    fetch_own = pltpu.make_async_copy(hamiltonian, own, sems.at[1])
+    fetch = pltpu.make_async_copy(density, rows, sems.at[ROWS])
+    fetch_own = pltpu.make_async_copy(hamiltonian, own, sems.at[ROWS + 1])
+    fetch_own.start()
     fetch.start()
-    fetch_own.start()
+    fetch_own.wait()
+    turned = pltpu.roll(own[...], (512 - 16 * group) & 511, 1)
+    lane = lax.broadcasted_iota(jnp.int32, (16, 128), 1)
+    block[:16] = jnp.where(lane < 16, 0.5 * turned[:, :128], turned[:, :128])
+    block[16:32] = turned[:, 128:256]
+    last = 0.5 * turned[:, 256:384]
+    lane = lax.broadcasted_iota(jnp.int32, (8, 128), 1)
+    block[32:] = jnp.where(lane < 16, last[:8], pltpu.roll(last[8:], 16, 1))
+    sends = [pltpu.make_async_copy(block, copies.at[r], sems.at[r]) for r in range(ROWS)]
+    for send in sends:
+        send.start()
     fetch.wait()
     for p in range(4):
         for j in range(4):
@@ -51,16 +68,8 @@
             picked = tiles[pl.ds(first + a, 16, stride=16), :]
             for p in range(4):
                 target[s & 3, 8 * p + 4 * a : 8 * p + 4 * a + 4, :] = picked[4 * p : 4 * p + 4]
-    fetch_own.wait()
-    turned = pltpu.roll(own[...], (512 - 16 * group) & 511, 1)
-    lane = lax.broadcasted_iota(jnp.int32, (16, 128), 1)
-    main = jnp.where(lane < 16, 0.5 * turned[:, :128], turned[:, :128])
-    last = 0.5 * turned[:, 256:384]
-    lane = lax.broadcasted_iota(jnp.int32, (8, 128), 1)
-    last = jnp.where(lane < 16, last[:8], pltpu.roll(last[8:], 16, 1))
-    block = jnp.concatenate([main, turned[:, 128:256], last], axis=0)
-    for r in range(ROWS):
-        copies[r] = block
+    for send in sends:
+        send.wait()
 
 
 def join_symmetric(blocks, upper):
@@ -100,7 +109,7 @@
         out[s - 1][1] = far_blocks[s]
 
 
-def prepare(levels, neighbours, decay, bath, couplings, codes, ints, floats, fields):
+def prepare_kernel(levels, neighbours, decay, bath, couplings, ints, floats, fields, codes):
     plane = my_plane()
     row = 16 * lax.axis_index("row").astype(jnp.int32) + 2 * plane
 
@@ -186,6 +195,29 @@
     return jnp.stack(parts)
 
 
+def early_kernel(ints_far, floats_far, fields, near_blocks, far_blocks, *refs):
+    *pairs, state, first, right, second, ints, floats, sems = refs
+    fetches = [
+        pltpu.make_async_copy(ints_far, ints, sems.at[0]),
+        pltpu.make_async_copy(floats_far, floats, sems.at[1]),
+    ]
+    for fetch in fetches:
+        fetch.start()
+    state[0:4] = near_blocks[0].reshape(4, 8, 128)
+    state[16:20] = far_blocks[0].reshape(4, 8, 128)
+    for s in range(1, 4):
+        state[4 * s : 4 * s + 4] = pairs[s - 1][0].reshape(4, 8, 128)
+        state[4 * s + 16 : 4 * s + 20] = pairs[s - 1][1].reshape(4, 8, 128)
+    right[...] = jnp.zeros_like(right)
+    for fetch in fetches:
+        fetch.wait()
+    first[...] = decayed(floats, state)
+    mix(ints, floats, fields, state, first, right)
+    first[...] = A2 * state[...] + A3 * first[...]
+    second[...] = decayed(floats, first)
+    mix(ints, floats, fields, first, second, None)
+
+
 def gather_rows(ref):
     return jnp.concatenate(
         [
@@ -235,26 +267,18 @@
     return value
 
 
-def rows_kernel(levels, neighbours, decay, bath, couplings, h, *refs):
-    near_blocks, far_blocks, *pairs, message, h_high, h_low = refs[:8]
-    codes, ints, floats, fields, state, first, right, second, rows, p, ep, bp, upper = refs[8:]
+def rows_kernel(ints_far, floats_far, fields, h, state, right, first, second, *refs):
+    message, h_high, h_low, ints, floats, rows, p, ep, bp, upper, sems = refs
     plane = my_plane()
-    prepare(levels, neighbours, decay, bath, couplings, codes, ints, floats, fields)
+    fetches = [
+        pltpu.make_async_copy(ints_far, ints, sems.at[0]),
+        pltpu.make_async_copy(floats_far, floats, sems.at[1]),
+    ]
+    for fetch in fetches:
+        fetch.start()
     high, low = halves(join_symmetric(h, upper))
     h_high[...] = high
     h_low[...] = low
-
-    state[0:4] = near_blocks[0].reshape(4, 8, 128)
-    state[16:20] = far_blocks[0].reshape(4, 8, 128)
-    for s in range(1, 4):
-        state[4 * s : 4 * s + 4] = pairs[s - 1][0].reshape(4, 8, 128)
-        state[4 * s + 16 : 4 * s + 20] = pairs[s - 1][1].reshape(4, 8, 128)
-    first[...] = decayed(floats, state)
-    right[...] = jnp.zeros_like(right)
-    mix(ints, floats, fields, state, first, right)
-    first[...] = A2 * state[...] + A3 * first[...]
-    second[...] = decayed(floats, first)
-    mix(ints, floats, fields, first, second, None)
 
     def product(value):
         count = value.shape[0]
@@ -283,6 +307,8 @@
     (p_value,) = apply([s_value])
     p[...] = p_value
     v1, edge = apply([first[...] + A3 * p_value, p_value + right[...]])
+    for fetch in fetches:
+        fetch.wait()
     damped = decayed(floats, p)
     ep[...] = damped
     bp[...] = damped + edge
@@ -345,18 +371,23 @@
 def on_device(density, hamiltonian, couplings, decay_rates, bath_coeffs, levels, neighbours):
     copies, near_blocks, far_blocks = pl.pallas_call(
         split_kernel,
-        out_shape=[f32(ROWS, 40, 128), f32(4, 32, 128), f32(4, 32, 128)],
-        in_specs=[ANY] * 2,
-        out_specs=[VMEM] * 3,
+        out_shape=[
+            pltpu.HBM((ROWS, 40, 128), jnp.float32),
+            f32(4, 32, 128),
+            f32(4, 32, 128),
+        ],
+        in_specs=[HBM] * 2,
+        out_specs=[HBM] + [VMEM] * 2,
         scratch_shapes=[
             pltpu.VMEM((4, 16, 512), jnp.float32),
             pltpu.VMEM((16, 512), jnp.float32),
+            pltpu.VMEM((40, 128), jnp.float32),
             pltpu.VMEM((256, 128), jnp.float32),
-            pltpu.SemaphoreType.DMA((2,)),
+            pltpu.SemaphoreType.DMA((ROWS + 2,)),
         ],
         name="split",
         compiler_params=PARAMS,
-    )(density.reshape(4, 16, 512), hamiltonian)
+    )(*far(density.reshape(4, 16, 512), hamiltonian))
     blocks = lax.all_to_all(copies, "row", 0, 0, tiled=True)
 
     def swap(block, s):
@@ -375,31 +406,50 @@
 
     bf16 = pltpu.VMEM((512, 512), jnp.bfloat16)
     whole = pltpu.VMEM((32, 8, 128), jnp.float32)
+    ints, floats, fields = pl.pallas_call(
+        prepare_kernel,
+        out_shape=[
+            jax.ShapeDtypeStruct((4, EDGES), jnp.int32),
+            jax.ShapeDtypeStruct((3, EDGES), jnp.float32),
+            f32(3, 64, 128),
+        ],
+        in_specs=[SMEM] * 4 + [VMEM],
+        out_specs=[SMEM] * 2 + [VMEM],
+        scratch_shapes=[pltpu.SMEM((EDGES,), jnp.int32)],
+        name="prepare",
+        compiler_params=PARAMS,
+    )(levels.T, jnp.swapaxes(neighbours, 1, 2), decay_rates, bath_coeffs, couplings)
+
+    state, first, right, second = pl.pallas_call(
+        early_kernel,
+        out_shape=[whole] * 4,
+        in_specs=[ANY] * 2 + [VMEM] * 6,
+        out_specs=[VMEM] * 4,
+        scratch_shapes=[
+            pltpu.SMEM((4, EDGES), jnp.int32),
+            pltpu.SMEM((3, EDGES), jnp.float32),
+            pltpu.SemaphoreType.DMA((2,)),
+        ],
+        name="early",
+        compiler_params=PARAMS,
+    )(ints, floats, *near(fields, near_blocks, far_blocks, *pairs))
+
     message, h_high, h_low = pl.pallas_call(
         rows_kernel,
         out_shape=[f32(512, 128), bf16, bf16],
-        in_specs=[SMEM] * 4 + [VMEM] * 7,
+        in_specs=[ANY] * 2 + [VMEM] * 6,
         out_specs=[VMEM] * 3,
         scratch_shapes=[
-            pltpu.SMEM((EDGES,), jnp.int32),
             pltpu.SMEM((4, EDGES), jnp.int32),
             pltpu.SMEM((3, EDGES), jnp.float32),
-            pltpu.VMEM((3, 64, 128), jnp.float32),
-            *[whole] * 4,
             pltpu.VMEM((256, 128), jnp.float32),
             *[whole] * 3,
             pltpu.VMEM((512, 512), jnp.float32),
+            pltpu.SemaphoreType.DMA((2,)),
         ],
         name="rows",
         compiler_params=PARAMS,
-    )(
-        levels.T,
-        jnp.swapaxes(neighbours, 1, 2),
-        decay_rates,
-        bath_coeffs,
-        couplings,
-        *near(blocks, near_blocks, far_blocks, *pairs),
-    )
+    )(ints, floats, *near(fields, blocks, state, right, first, second))
 
     received = lax.all_to_all(
         message.reshape(256, 2, 128), ("row", "hier"), 0, 0, tiled=True

time: 78.4 us -> 76.1 us (0.971)
  waiting for transfers between devices: 13.8 us -> 10.7 us
  Pallas kernels: 8.36 us -> 10.8 us
  local copies, waits for them, and re-layouts: 2.33 us -> 0.68 us
    pallas_call x1 -> x3, Pallas kernels: 1.26 us -> 5.87 us  [the longest x1 2.37 us: on_device(): pl.pallas_call(prepare_kernel, out_shape=[jax.ShapeDtypeStruct((4, EDGES)...]
    ppermute x4, waiting for transfers between devices: 6.14 us -> 3.07 us  [swap(): return lax.ppermute(block, 'hier', [(i, i ^ s) for i in range(PLANES)])]
    pallas_call x1, Pallas kernels: 4.81 us -> 2.64 us  [on_device(): pl.pallas_call(rows_kernel, out_shape=[f32(512, 128), bf16, bf16], in_spe...]
    unnamed x16 -> x12, local copies, waits for them, and re-layouts: 2.33 us -> 0.68 us
  transfers between devices with their start and end apart: 6 -> 6, of which waited for: 4 -> 3; matrix products, arithmetic and copies ran while one was open for 0% -> 0% of each run, Pallas kernels for 0% -> 5%
where the time goes in v1:
time: 76.1 us; the launch traced here: 75.8 us
  blocking collectives  29.9 us (39%)
  starting transfers between devices  23.6 us (31%)
  Pallas kernels  10.8 us (14%)
  waiting for transfers between devices  10.7 us (14%)
    all_to_all x1, blocking collectives, on_device(): lax.all_to_all(message.reshape(256, 2, 128), ('row', 'hier'), 0, 0, tiled...  29.9 us
    ppermute x4, starting transfers between devices, swap(): return lax.ppermute(block, 'hier', [(i, i ^ s) for i in range(PLANES)])  10.6 us
    all_to_all x1, starting transfers between devices, on_device(): blocks = lax.all_to_all(copies, 'row', 0, 0, tiled=True)  8.59 us
    all_to_all x1, waiting for transfers between devices, on_device(): lax.all_to_all(message.reshape(ROWS, 8, 128), 'row', 0, 0, tiled=True)  7.65 us
    all_to_all x1, starting transfers between devices, on_device(): lax.all_to_all(message.reshape(ROWS, 8, 128), 'row', 0, 0, tiled=True)  4.36 us
    ppermute x4, waiting for transfers between devices, swap(): return lax.ppermute(block, 'hier', [(i, i ^ s) for i in range(PLANES)])  3.07 us
    pallas_call x1, Pallas kernels, on_device(): pl.pallas_call(rows_kernel, out_shape=[f32(512, 128), bf16, bf16], in_spe...  2.64 us
    pallas_call x1, Pallas kernels, on_device(): pl.pallas_call(prepare_kernel, out_shape=[jax.ShapeDtypeStruct((4, EDGES)...  2.37 us
  transfers between devices with their start and end apart: 6, of which 3 were waited for; matrix products, arithmetic and copies ran while one was open for 0% of the time, Pallas kernels for 5%

profile of v1, /device:TPU:1, one launch (start us, length us, event | category | flops | bytes accessed | tf_op | source)
XLA Modules:
  0.0 75.8 jit_solution(16050992596453668031)
XLA Ops:
  0.0 2.1 %split.1 = (f32[32,40,128]{2,1,0:T(8,128)}, f32[4,32,128]{2,1,0:T(8,128)S(1)}, f32[4,32,128]{2,1,0:T(8,128)S(1)}) custom-call(f32[4,16,512]{2,1,0:T(8,128)} %bitcast.11, f32[16,512]{1,0:T(8,128)} %hamiltonian.1), custom_call_target="tpu_custom_call" | custom-call | tf_op jit(solution)/shard_map/split/pallas_call | solution.py:372
  2.1 8.6 %all-to-all-start = ((f32[32,40,128]{2,1,0:T(8,128)}), f32[32,40,128]{2,1,0:T(8,128)S(1)}, u32[]{:S(2)}, u32[]{:S(2)}) async-start(f32[32,40,128]{2,1,0:T(8,128)} %get-tuple-element.26), calls=%async_computation | async-start | bytes 1310720 | tf_op jit(solution)/shard_map/all_to_all | solution.py:391
  10.7 7.0 %collective-permute-start = (f32[4,32,128]{2,1,0:T(8,128)S(1)}, f32[4,32,128]{2,1,0:T(8,128)S(1)}, u32[]{:S(2)}, u32[]{:S(2)}) collective-permute-start(f32[4,32,128]{2,1,0:T(8,128)S(1)} %get-tuple-element.28), channel_id=1, source_target_pairs={{0,128},{32,160},{64,192},{96,224},{128,0},{160,32},{192,64},{224,... | collective-permute-start | bytes 196616 | tf_op jit(solution)/shard_map/ppermute | solution.py:394
  17.7 2.2 %collective-permute-done.far_blocks = f32[4,32,128]{2,1,0:T(8,128)S(1)} collective-permute-done((f32[4,32,128]{2,1,0:T(8,128)S(1)}, f32[4,32,128]{2,1,0:T(8,128)S(1)}, u32[]{:S(2)}, u32[]{:S(2)}) %collective-permute-start) | collective-permute-done | bytes 65568 | tf_op jit(solution)/shard_map/ppermute | solution.py:394
  19.9 0.0 copy-start.1
  19.9 0.0 copy-start.3
  19.9 0.0 copy-start.5
  19.9 0.0 copy-start.2
  19.9 0.8 %collective-permute-start.1 = (f32[2,32,128]{2,1,0:T(8,128)S(1)}, f32[2,32,128]{2,1,0:T(8,128)S(1)}, u32[]{:S(2)}, u32[]{:S(2)}) collective-permute-start(f32[2,32,128]{2,1,0:T(8,128)S(1)} %get-tuple-element.29), channel_id=1, source_target_pairs={{0,32},{32,0},{64,96},{96,64},{128,160},{160,128},{192,224},{224,1... | collective-permute-start | bytes 98312 | tf_op jit(solution)/shard_map/ppermute | solution.py:394
  20.7 2.1 %collective-permute-start.2 = (f32[2,32,128]{2,1,0:T(8,128)S(1)}, f32[2,32,128]{2,1,0:T(8,128)S(1)}, u32[]{:S(2)}, u32[]{:S(2)}) collective-permute-start(f32[2,32,128]{2,1,0:T(8,128)S(1)} %get-tuple-element.30), channel_id=1, source_target_pairs={{0,64},{32,96},{64,0},{96,32},{128,192},{160,224},{192,128},{224,1... | collective-permute-start | bytes 98312 | tf_op jit(solution)/shard_map/ppermute | solution.py:394
  22.8 0.7 collective-permute-start.3
  23.6 0.0 copy-start.4
  23.6 0.0 copy-done.1
  23.6 0.0 copy-done.3
  23.6 0.0 copy-done.5
  23.6 0.0 copy-done.2
  23.6 0.7 copy-done.4
  24.2 2.4 %prepare.1 = (s32[4,264]{1,0:T(4,128)S(1)}, f32[3,264]{1,0:T(4,128)S(1)}, f32[3,64,128]{2,1,0:T(8,128)S(1)}) custom-call(s32[8,16]{1,0:T(8,128)S(1)} %bitcast.15, s32[2,8,16]{2,1,0:T(8,128)S(1)} %bitcast.14, f32[8]{0:T(128)S(1)} %copy-done.5, f32[2,8]{1,0:T(2,128)S(1)} %copy-done.4, f32[8,512]{1,0:T(8,128)S(1)} %copy-done.1), custom_call_target="tpu_custom_call" | custom-call | tf_op jit(solution)/shard_map/prepare/pallas_call | solution.py:409
  26.6 0.0 collective-permute-done.1.refs_0_
  26.6 0.0 collective-permute-done.2.refs_1_
  26.6 0.8 %collective-permute-done.3.refs_2_ = f32[2,32,128]{2,1,0:T(8,128)S(1)} collective-permute-done((f32[2,32,128]{2,1,0:T(8,128)S(1)}, f32[2,32,128]{2,1,0:T(8,128)S(1)}, u32[]{:S(2)}, u32[]{:S(2)}) %collective-permute-start.3) | collective-permute-done | bytes 32800 | tf_op jit(solution)/shard_map/ppermute | solution.py:394
  27.5 1.4 %early.1 = (f32[32,8,128]{2,1,0:T(8,128)S(1)}, f32[32,8,128]{2,1,0:T(8,128)S(1)}, f32[32,8,128]{2,1,0:T(8,128)S(1)}, f32[32,8,128]{2,1,0:T(8,128)S(1)}) custom-call(s32[4,264]{1,0:T(4,128)S(1)} %get-tuple-element.23.ints_far, f32[3,264]{1,0:T(4,128)S(1)} %get-tuple-element.24.floats_far, f32[3,64,128]{2,1,0:T(8,128)S(1)} %get-tuple-element.25.fields, ...), custom_call_target="tpu_custom_call" | custom-call | tf_op jit(solution)/shard_map/early/pallas_call | solution.py:423
  28.9 0.0 all-to-all-done.h
  28.9 2.6 %rows.1 = (f32[512,128]{1,0:T(8,128)S(1)}, bf16[512,512]{1,0:T(8,128)(2,1)S(1)}, bf16[512,512]{1,0:T(8,128)(2,1)S(1)}) custom-call(s32[4,264]{1,0:T(4,128)S(1)} %get-tuple-element.23.ints_far, f32[3,264]{1,0:T(4,128)S(1)} %get-tuple-element.24.floats_far, f32[3,64,128]{2,1,0:T(8,128)S(1)} %get-tuple-element.25.fields, f32[32,40,128]{2,1,0:T(8,128)S(1)} %all-to-all-done.h, ...), custom_call_target="tpu_custom_call" | custom-call | tf_op jit(solution)/shard_map/rows/pallas_call | solution.py:437
  31.6 29.9 %all_to_all.15 = f32[256,2,128]{2,1,0:T(2,128)S(1)} all-to-all(f32[256,2,128]{2,1,0:T(2,128)S(1)} %bitcast.13), channel_id=1, replica_groups=mesh['hier'=8,'row'=32] {'row','hier'}, dimensions={0} | all-to-all | bytes 524288 | tf_op jit(solution)/shard_map/all_to_all | solution.py:454
  61.4 1.2 %columns.1 = (f32[256,128]{1,0:T(8,128)}, f32[512,128]{1,0:T(8,128)S(1)}) custom-call(f32[512,128]{1,0:T(8,128)S(1)} %bitcast.9, bf16[512,512]{1,0:T(8,128)(2,1)S(1)} %get-tuple-element.37.h_high, bf16[512,512]{1,0:T(8,128)(2,1)S(1)} %get-tuple-element.38.h_low), custom_call_target="tpu_custom_call" | custom-call | tf_op jit(solution)/shard_map/columns/pallas_call | solution.py:458
  62.7 0.0 copy-start
  62.7 4.4 %all-to-all-start.2 = ((f32[32,8,128]{2,1,0:T(8,128)}), f32[32,8,128]{2,1,0:T(8,128)S(1)}, u32[]{:S(2)}, u32[]{:S(2)}) async-start(f32[32,8,128]{2,1,0:T(8,128)} %bitcast.6), calls=%async_computation.2 | async-start | bytes 262144 | tf_op jit(solution)/shard_map/all_to_all | solution.py:467
  67.0 0.0 copy-done
  67.1 0.1 base.1
  67.2 7.7 %all-to-all-done.2 = f32[32,8,128]{2,1,0:T(8,128)S(1)} async-done(((f32[32,8,128]{2,1,0:T(8,128)}), f32[32,8,128]{2,1,0:T(8,128)S(1)}, u32[]{:S(2)}, u32[]{:S(2)}) %all-to-all-start.2) | async-done | bytes 131104 | tf_op jit(solution)/shard_map/all_to_all | solution.py:467
  74.8 0.9 %finish.1 = f32[64,512]{1,0:T(8,128)} custom-call(f32[64,512]{1,0:T(8,128)S(1)} %base.1, f32[256,128]{1,0:T(8,128)S(1)} %bitcast.10), custom_call_target="tpu_custom_call" | custom-call | tf_op jit(solution)/shard_map/finish/pallas_call | solution.py:475
  (1 shorter events, 0.0 us)
Async XLA Ops:
  2.1 26.9 %all-to-all-start = ((f32[32,40,128]{2,1,0:T(8,128)}), f32[32,40,128]{2,1,0:T(8,128)S(1)}, u32[]{:S(2)}, u32[]{:S(2)}) async-start(f32[32,40,128]{2,1,0:T(8,128)} %get-tuple-element.26), calls=%async_computation | async-start | bytes 1310720 | tf_op jit(solution)/shard_map/all_to_all | solution.py:391
  10.7 9.2 %collective-permute-start = (f32[4,32,128]{2,1,0:T(8,128)S(1)}, f32[4,32,128]{2,1,0:T(8,128)S(1)}, u32[]{:S(2)}, u32[]{:S(2)}) collective-permute-start(f32[4,32,128]{2,1,0:T(8,128)S(1)} %get-tuple-element.28), channel_id=1, source_target_pairs={{0,128},{32,160},{64,192},{96,224},{128,0},{160,32},{192,64},{224,... | collective-permute-start | bytes 196616 | tf_op jit(solution)/shard_map/ppermute | solution.py:394
  19.9 3.7 %copy-start.1 = (f32[8,512]{1,0:T(8,128)S(1)}, f32[8,512]{1,0:T(8,128)}, u32[]{:S(2)}) copy-start(f32[8,512]{1,0:T(8,128)} %couplings.1) | copy-start | bytes 49156
  19.9 3.7 %copy-start.3 = (s32[16,8]{0,1:T(8,128)S(1)}, s32[16,8]{0,1:T(8,128)}, u32[]{:S(2)}) copy-start(s32[16,8]{0,1:T(8,128)} %param.12) | copy-start | bytes 1540
  19.9 3.7 %copy-start.5 = (f32[8]{0:T(128)S(1)}, f32[8]{0:T(128)}, u32[]{:S(2)}) copy-start(f32[8]{0:T(128)} %decay.1) | copy-start | bytes 100
  19.9 3.7 %copy-start.2 = (s32[2,16,8]{1,2,0:T(8,128)S(1)}, s32[2,16,8]{1,2,0:T(8,128)}, u32[]{:S(2)}) copy-start(s32[2,16,8]{1,2,0:T(8,128)} %param.13) | copy-start | bytes 3076
  19.9 6.7 %collective-permute-start.1 = (f32[2,32,128]{2,1,0:T(8,128)S(1)}, f32[2,32,128]{2,1,0:T(8,128)S(1)}, u32[]{:S(2)}, u32[]{:S(2)}) collective-permute-start(f32[2,32,128]{2,1,0:T(8,128)S(1)} %get-tuple-element.29), channel_id=1, source_target_pairs={{0,32},{32,0},{64,96},{96,64},{128,160},{160,128},{192,224},{224,1... | collective-permute-start | bytes 98312 | tf_op jit(solution)/shard_map/ppermute | solution.py:394
  20.7 5.9 %collective-permute-start.2 = (f32[2,32,128]{2,1,0:T(8,128)S(1)}, f32[2,32,128]{2,1,0:T(8,128)S(1)}, u32[]{:S(2)}, u32[]{:S(2)}) collective-permute-start(f32[2,32,128]{2,1,0:T(8,128)S(1)} %get-tuple-element.30), channel_id=1, source_target_pairs={{0,64},{32,96},{64,0},{96,32},{128,192},{160,224},{192,128},{224,1... | collective-permute-start | bytes 98312 | tf_op jit(solution)/shard_map/ppermute | solution.py:394
  22.8 4.6 %collective-permute-start.3 = (f32[2,32,128]{2,1,0:T(8,128)S(1)}, f32[2,32,128]{2,1,0:T(8,128)S(1)}, u32[]{:S(2)}, u32[]{:S(2)}) collective-permute-start(f32[2,32,128]{2,1,0:T(8,128)S(1)} %get-tuple-element.31), channel_id=1, source_target_pairs={{0,96},{32,64},{64,32},{96,0},{128,224},{160,192},{192,160},{224,1... | collective-permute-start | bytes 98312 | tf_op jit(solution)/shard_map/ppermute | solution.py:394
  23.6 0.7 copy-start.4
  62.7 4.4 %copy-start = (f32[2,2,16,512]{3,2,1,0:T(8,128)S(1)}, f32[2,2,16,512]{3,2,1,0:T(8,128)}, u32[]{:S(2)}) copy-start(f32[2,2,16,512]{3,2,1,0:T(8,128)} %param.7) | copy-start | bytes 393220
  62.7 12.2 %all-to-all-start.2 = ((f32[32,8,128]{2,1,0:T(8,128)}), f32[32,8,128]{2,1,0:T(8,128)S(1)}, u32[]{:S(2)}, u32[]{:S(2)}) async-start(f32[32,8,128]{2,1,0:T(8,128)} %bitcast.6), calls=%async_computation.2 | async-start | bytes 262144 | tf_op jit(solution)/shard_map/all_to_all | solution.py:467

commit v2 on v1

--- a/solution.py
+++ b/solution.py
@@ -11,7 +11,8 @@
 A3 = A2 * time_step / 3
 
 PLANES = 8
-ROWS = 32
+CHIPS = 16
+SAME_CORE = [list(range(core, 2 * CHIPS, 2)) for core in range(2)]
 EDGES = 264
 
 
@@ -38,14 +39,21 @@
     return lax.axis_index("hier").astype(jnp.int32)
 
 
-def split_kernel(density, hamiltonian, copies, near_blocks, far_blocks, *scratch):
-    rows, own, block, tiles, sems = scratch
+def split_kernel(density, hamiltonian, *refs):
+    tables, (copies, near_blocks, far_blocks), held = refs[:5], refs[5:8], refs[8:13]
+    rows, own, block, tiles, sems = refs[13:]
     plane = my_plane()
     group = lax.axis_index("row").astype(jnp.int32)
-    fetch = pltpu.make_async_copy(density, rows, sems.at[ROWS])
-    fetch_own = pltpu.make_async_copy(hamiltonian, own, sems.at[ROWS + 1])
+    fetch = pltpu.make_async_copy(density, rows, sems.at[CHIPS])
+    fetch_own = pltpu.make_async_copy(hamiltonian, own, sems.at[CHIPS + 1])
     fetch_own.start()
     fetch.start()
+    loads = [
+        pltpu.make_async_copy(table, place, sems.at[CHIPS + 2 + i])
+        for i, (table, place) in enumerate(zip(tables, held))
+    ]
+    for load in loads:
+        load.start()
     fetch_own.wait()
     turned = pltpu.roll(own[...], (512 - 16 * group) & 511, 1)
     lane = lax.broadcasted_iota(jnp.int32, (16, 128), 1)
@@ -54,7 +62,7 @@
     last = 0.5 * turned[:, 256:384]
     lane = lax.broadcasted_iota(jnp.int32, (8, 128), 1)
     block[32:] = jnp.where(lane < 16, last[:8], pltpu.roll(last[8:], 16, 1))
-    sends = [pltpu.make_async_copy(block, copies.at[r], sems.at[r]) for r in range(ROWS)]
+    sends = [pltpu.make_async_copy(block, copies.at[r], sems.at[r]) for r in range(CHIPS)]
     for send in sends:
         send.start()
     fetch.wait()
@@ -68,19 +76,25 @@
             picked = tiles[pl.ds(first + a, 16, stride=16), :]
             for p in range(4):
                 target[s & 3, 8 * p + 4 * a : 8 * p + 4 * a + 4, :] = picked[4 * p : 4 * p + 4]
-    for send in sends:
-        send.wait()
-
-
-def join_symmetric(blocks, upper):
+    for wait in sends + loads:
+        wait.wait()
+
+
+def join_symmetric(mine, other, upper):
     lane = lax.broadcasted_iota(jnp.int32, (8, 128), 1)
-    for r in range(ROWS):
+    even = (lax.axis_index("row") & 1) == 0
+    for r in range(2 * CHIPS):
         tile, offset = r // 8, 16 * (r % 8)
+
+        def part(at):
+            pair = (mine[r // 2, at : at + 8, :], other[r // 2, at : at + 8, :])
+            return jnp.where(even, pair[r % 2], pair[1 - r % 2])
+
         for half in range(2):
             at = 8 * half
-            first = blocks[r, at : at + 8, :]
-            second = blocks[r, 16 + at : 24 + at, :]
-            last = blocks[r, 32:40, :]
+            first = part(at)
+            second = part(16 + at)
+            last = part(32)
             if offset:
                 first = pltpu.roll(first, offset, 1)
                 second = pltpu.roll(second, offset, 1)
@@ -101,6 +115,12 @@
                 upper[16 * r + at : 16 * r + at + 8, col : col + 128] = parts[i]
     value = upper[...]
     return value + jnp.transpose(value)
+
+
+def sites_kernel(mine, other, h_high, h_low, upper):
+    high, low = halves(join_symmetric(mine, other, upper))
+    h_high[...] = high
+    h_low[...] = low
 
 
 def pack_kernel(near_blocks, far_blocks, *out):
@@ -195,29 +215,6 @@
     return jnp.stack(parts)
 
 
-def early_kernel(ints_far, floats_far, fields, near_blocks, far_blocks, *refs):
-    *pairs, state, first, right, second, ints, floats, sems = refs
-    fetches = [
-        pltpu.make_async_copy(ints_far, ints, sems.at[0]),
-        pltpu.make_async_copy(floats_far, floats, sems.at[1]),
-    ]
-    for fetch in fetches:
-        fetch.start()
-    state[0:4] = near_blocks[0].reshape(4, 8, 128)
-    state[16:20] = far_blocks[0].reshape(4, 8, 128)
-    for s in range(1, 4):
-        state[4 * s : 4 * s + 4] = pairs[s - 1][0].reshape(4, 8, 128)
-        state[4 * s + 16 : 4 * s + 20] = pairs[s - 1][1].reshape(4, 8, 128)
-    right[...] = jnp.zeros_like(right)
-    for fetch in fetches:
-        fetch.wait()
-    first[...] = decayed(floats, state)
-    mix(ints, floats, fields, state, first, right)
-    first[...] = A2 * state[...] + A3 * first[...]
-    second[...] = decayed(floats, first)
-    mix(ints, floats, fields, first, second, None)
-
-
 def gather_rows(ref):
     return jnp.concatenate(
         [
@@ -267,8 +264,8 @@
     return value
 
 
-def rows_kernel(ints_far, floats_far, fields, h, state, right, first, second, *refs):
-    message, h_high, h_low, ints, floats, rows, p, ep, bp, upper, sems = refs
+def rows_kernel(ints_far, floats_far, fields, h_high, h_low, near_blocks, far_blocks, *refs):
+    *pairs, message, ints, floats, rows, state, first, right, second, p, ep, bp, sems = refs
     plane = my_plane()
     fetches = [
         pltpu.make_async_copy(ints_far, ints, sems.at[0]),
@@ -276,9 +273,13 @@
     ]
     for fetch in fetches:
         fetch.start()
-    high, low = halves(join_symmetric(h, upper))
-    h_high[...] = high
-    h_low[...] = low
+    state[0:4] = near_blocks[0].reshape(4, 8, 128)
+    state[16:20] = far_blocks[0].reshape(4, 8, 128)
+    for s in range(1, 4):
+        state[4 * s : 4 * s + 4] = pairs[s - 1][0].reshape(4, 8, 128)
+        state[4 * s + 16 : 4 * s + 20] = pairs[s - 1][1].reshape(4, 8, 128)
+    right[...] = jnp.zeros_like(right)
+    high, low = h_high[...], h_low[...]
 
     def product(value):
         count = value.shape[0]
@@ -306,9 +307,14 @@
     s_value = state[...]
     (p_value,) = apply([s_value])
     p[...] = p_value
-    v1, edge = apply([first[...] + A3 * p_value, p_value + right[...]])
     for fetch in fetches:
         fetch.wait()
+    first[...] = decayed(floats, state)
+    mix(ints, floats, fields, state, first, right)
+    first[...] = A2 * state[...] + A3 * first[...]
+    second[...] = decayed(floats, first)
+    mix(ints, floats, fields, first, second, None)
+    v1, edge = apply([first[...] + A3 * p_value, p_value + right[...]])
     damped = decayed(floats, p)
     ep[...] = damped
     bp[...] = damped + edge
@@ -369,26 +375,29 @@
 
 
 def on_device(density, hamiltonian, couplings, decay_rates, bath_coeffs, levels, neighbours):
-    copies, near_blocks, far_blocks = pl.pallas_call(
+    tables = (levels.T, jnp.swapaxes(neighbours, 1, 2), decay_rates, bath_coeffs, couplings)
+    copies, near_blocks, far_blocks, *tables = pl.pallas_call(
         split_kernel,
         out_shape=[
-            pltpu.HBM((ROWS, 40, 128), jnp.float32),
+            pltpu.HBM((CHIPS, 40, 128), jnp.float32),
             f32(4, 32, 128),
             f32(4, 32, 128),
+            *[pltpu.VMEM(table.shape, table.dtype) for table in tables],
         ],
-        in_specs=[HBM] * 2,
-        out_specs=[HBM] + [VMEM] * 2,
+        in_specs=[HBM] * 7,
+        out_specs=[HBM] + [VMEM] * 7,
         scratch_shapes=[
             pltpu.VMEM((4, 16, 512), jnp.float32),
             pltpu.VMEM((16, 512), jnp.float32),
             pltpu.VMEM((40, 128), jnp.float32),
             pltpu.VMEM((256, 128), jnp.float32),
-            pltpu.SemaphoreType.DMA((ROWS + 2,)),
+            pltpu.SemaphoreType.DMA((CHIPS + 7,)),
         ],
         name="split",
         compiler_params=PARAMS,
-    )(*far(density.reshape(4, 16, 512), hamiltonian))
-    blocks = lax.all_to_all(copies, "row", 0, 0, tiled=True)
+    )(*far(density.reshape(4, 16, 512), hamiltonian, *tables))
+    mine = lax.all_to_all(copies, "row", 0, 0, axis_index_groups=SAME_CORE, tiled=True)
+    other = lax.ppermute(mine, "row", [(i, i ^ 1) for i in range(2 * CHIPS)])
 
     def swap(block, s):
         return lax.ppermute(block, "hier", [(i, i ^ s) for i in range(PLANES)])
@@ -402,7 +411,7 @@
         name="pack",
         compiler_params=PARAMS,
     )(*near(near_blocks, far_blocks))
-    pairs = [swap(packed[s - 1], s) for s in (1, 2, 3)]
+    pairs = [swap(packed[s - 1], s) for s in (3, 2, 1)][::-1]
 
     bf16 = pltpu.VMEM((512, 512), jnp.bfloat16)
     whole = pltpu.VMEM((32, 8, 128), jnp.float32)
@@ -418,38 +427,33 @@
         scratch_shapes=[pltpu.SMEM((EDGES,), jnp.int32)],
         name="prepare",
         compiler_params=PARAMS,
-    )(levels.T, jnp.swapaxes(neighbours, 1, 2), decay_rates, bath_coeffs, couplings)
-
-    state, first, right, second = pl.pallas_call(
-        early_kernel,
-        out_shape=[whole] * 4,
-        in_specs=[ANY] * 2 + [VMEM] * 6,
-        out_specs=[VMEM] * 4,
-        scratch_shapes=[
-            pltpu.SMEM((4, EDGES), jnp.int32),
-            pltpu.SMEM((3, EDGES), jnp.float32),
-            pltpu.SemaphoreType.DMA((2,)),
-        ],
-        name="early",
-        compiler_params=PARAMS,
-    )(ints, floats, *near(fields, near_blocks, far_blocks, *pairs))
-
-    message, h_high, h_low = pl.pallas_call(
+    )(*tables[:4], *near(tables[4]))
+
+    h_high, h_low = pl.pallas_call(
+        sites_kernel,
+        out_shape=[bf16, bf16],
+        in_specs=[VMEM] * 2,
+        out_specs=[VMEM] * 2,
+        scratch_shapes=[pltpu.VMEM((512, 512), jnp.float32)],
+        name="sites",
+        compiler_params=PARAMS,
+    )(*near(mine, other))
+
+    message = pl.pallas_call(
         rows_kernel,
-        out_shape=[f32(512, 128), bf16, bf16],
-        in_specs=[ANY] * 2 + [VMEM] * 6,
-        out_specs=[VMEM] * 3,
+        out_shape=f32(512, 128),
+        in_specs=[ANY] * 2 + [VMEM] * 8,
+        out_specs=VMEM,
         scratch_shapes=[
             pltpu.SMEM((4, EDGES), jnp.int32),
             pltpu.SMEM((3, EDGES), jnp.float32),
             pltpu.VMEM((256, 128), jnp.float32),
-            *[whole] * 3,
-            pltpu.VMEM((512, 512), jnp.float32),
+            *[whole] * 7,
             pltpu.SemaphoreType.DMA((2,)),
         ],
         name="rows",
         compiler_params=PARAMS,
-    )(ints, floats, *near(fields, blocks, state, right, first, second))
+    )(ints, floats, *near(fields, h_high, h_low, near_blocks, far_blocks, *pairs))
 
     received = lax.all_to_all(
         message.reshape(256, 2, 128), ("row", "hier"), 0, 0, tiled=True
@@ -465,7 +469,7 @@
     )(*near(received, h_high, h_low))
 
     received = lax.all_to_all(
-        message.reshape(ROWS, 8, 128), "row", 0, 0, tiled=True
+        message.reshape(2 * CHIPS, 8, 128), "row", 0, 0, tiled=True
     ).reshape(256, 128)
 
     base = pl.pallas_call(

time: 76.1 us -> 80.8 us (1.062)
  blocking collectives: 29.9 us -> 41.9 us
  starting transfers between devices: 23.6 us -> 17.4 us
    all_to_all x0 -> x1, blocking collectives: none -> 15.4 us  [on_device(): lax.all_to_all(copies, 'row', 0, 0, axis_index_groups=SAME_CORE, tiled=True)]
    all_to_all x2 -> x1, starting transfers between devices: 12.9 us -> 4.36 us  [on_device(): lax.all_to_all(message.reshape(2 * CHIPS, 8, 128), 'row', 0, 0, tiled=True)]
    all_to_all x1, blocking collectives: 29.9 us -> 26.5 us  [on_device(): lax.all_to_all(message.reshape(256, 2, 128), ('row', 'hier'), 0, 0, tiled...]
    ppermute x0 -> x1, starting transfers between devices: none -> 2.27 us  [on_device(): other = lax.ppermute(mine, 'row', [(i, i ^ 1) for i in range(2 * CHIPS)])]
    all_to_all x2 -> x1, waiting for transfers between devices: 7.66 us -> 7.65 us  [on_device(): lax.all_to_all(message.reshape(2 * CHIPS, 8, 128), 'row', 0, 0, tiled=True)]
  transfers between devices with their start and end apart: 6 -> 6, of which waited for: 3 -> 3; matrix products, arithmetic and copies ran while one was open for 0% -> 0% of each run, Pallas kernels for 5% -> 4%
where the time goes in v2:
time: 80.8 us; the launch traced here: 80.5 us
  blocking collectives  41.9 us (52%)
  starting transfers between devices  17.4 us (22%)
  waiting for transfers between devices  10.8 us (13%)
  Pallas kernels  10.3 us (13%)
    all_to_all x1, blocking collectives, on_device(): lax.all_to_all(message.reshape(256, 2, 128), ('row', 'hier'), 0, 0, tiled...  26.5 us
    all_to_all x1, blocking collectives, on_device(): lax.all_to_all(copies, 'row', 0, 0, axis_index_groups=SAME_CORE, tiled=True)  15.4 us
    ppermute x4, starting transfers between devices, swap(): return lax.ppermute(block, 'hier', [(i, i ^ s) for i in range(PLANES)])  10.8 us
    all_to_all x1, waiting for transfers between devices, on_device(): lax.all_to_all(message.reshape(2 * CHIPS, 8, 128), 'row', 0, 0, tiled=True)  7.65 us
    all_to_all x1, starting transfers between devices, on_device(): lax.all_to_all(message.reshape(2 * CHIPS, 8, 128), 'row', 0, 0, tiled=True)  4.36 us
    pallas_call x1, Pallas kernels, on_device(): pl.pallas_call(rows_kernel, out_shape=f32(512, 128), in_specs=[ANY] * 2 +...  3.32 us
    ppermute x4, waiting for transfers between devices, swap(): return lax.ppermute(block, 'hier', [(i, i ^ s) for i in range(PLANES)])  3.18 us
    pallas_call x1, Pallas kernels, on_device(): pl.pallas_call(prepare_kernel, out_shape=[jax.ShapeDtypeStruct((4, EDGES)...  2.37 us
  transfers between devices with their start and end apart: 6, of which 3 were waited for; matrix products, arithmetic and copies ran while one was open for 0% of the time, Pallas kernels for 4%

profile of v2, /device:TPU:1, one launch (start us, length us, event | category | flops | bytes accessed | tf_op | source)
XLA Modules:
  0.0 80.5 jit_solution(6632516565109884721)
XLA Ops:
  0.0 1.8 %split.1 = (f32[16,40,128]{2,1,0:T(8,128)}, f32[4,32,128]{2,1,0:T(8,128)S(1)}, f32[4,32,128]{2,1,0:T(8,128)S(1)}, s32[8,16]{1,0:T(8,128)S(1)}, s32[2,8,16]{2,1,0...) custom-call(f32[4,16,512]{2,1,0:T(8,128)} %bitcast.12, f32[16,512]{1,0:T(8,128)} %hamiltonian.1, ...), custom_call_target="tpu_custom_call" | custom-call | tf_op jit(solution)/shard_map/split/pallas_call | solution.py:379
  1.8 15.4 %all_to_all.15.mine = f32[16,40,128]{2,1,0:T(8,128)S(1)} all-to-all(f32[16,40,128]{2,1,0:T(8,128)} %get-tuple-element.31), channel_id=1, replica_groups={{0,2,4,6,8,10,12,14,16,18,20,22,24,26,28,30},{1,3,5,7,9,11,13,15,17,19,..., dimensions={0} | all-to-all | bytes 655360 | tf_op jit(solution)/shard_map/all_to_all | solution.py:399
  17.3 2.3 %collective-permute-start = (f32[16,40,128]{2,1,0:T(8,128)S(1)}, f32[16,40,128]{2,1,0:T(8,128)S(1)}, u32[]{:S(2)}, u32[]{:S(2)}) collective-permute-start(f32[16,40,128]{2,1,0:T(8,128)S(1)} %all_to_all.15.mine), channel_id=1, source_target_pairs={{0,1},{1,0},{2,3},{3,2},{4,5},{5,4},{6,7},{7,6},{8,9},{9,8},{10,11... | collective-permute-start | bytes 983048 | tf_op jit(solution)/shard_map/ppermute | solution.py:400
  19.5 6.9 %collective-permute-start.1 = (f32[4,32,128]{2,1,0:T(8,128)S(1)}, f32[4,32,128]{2,1,0:T(8,128)S(1)}, u32[]{:S(2)}, u32[]{:S(2)}) collective-permute-start(f32[4,32,128]{2,1,0:T(8,128)S(1)} %get-tuple-element.35), channel_id=1, source_target_pairs={{0,128},{32,160},{64,192},{96,224},{128,0},{160,32},{192,64},{224,... | collective-permute-start | bytes 196616 | tf_op jit(solution)/shard_map/ppermute | solution.py:403
  26.5 2.5 %collective-permute-done.1.far_blocks = f32[4,32,128]{2,1,0:T(8,128)S(1)} collective-permute-done((f32[4,32,128]{2,1,0:T(8,128)S(1)}, f32[4,32,128]{2,1,0:T(8,128)S(1)}, u32[]{:S(2)}, u32[]{:S(2)}) %collective-permute-start.1) | collective-permute-done | bytes 65568 | tf_op jit(solution)/shard_map/ppermute | solution.py:403
  28.9 0.8 %collective-permute-start.2 = (f32[2,32,128]{2,1,0:T(8,128)S(1)}, f32[2,32,128]{2,1,0:T(8,128)S(1)}, u32[]{:S(2)}, u32[]{:S(2)}) collective-permute-start(f32[2,32,128]{2,1,0:T(8,128)S(1)} %get-tuple-element.36), channel_id=1, source_target_pairs={{0,32},{32,0},{64,96},{96,64},{128,160},{160,128},{192,224},{224,1... | collective-permute-start | bytes 98312 | tf_op jit(solution)/shard_map/ppermute | solution.py:403
  29.8 2.1 %collective-permute-start.3 = (f32[2,32,128]{2,1,0:T(8,128)S(1)}, f32[2,32,128]{2,1,0:T(8,128)S(1)}, u32[]{:S(2)}, u32[]{:S(2)}) collective-permute-start(f32[2,32,128]{2,1,0:T(8,128)S(1)} %get-tuple-element.37), channel_id=1, source_target_pairs={{0,64},{32,96},{64,0},{96,32},{128,192},{160,224},{192,128},{224,1... | collective-permute-start | bytes 98312 | tf_op jit(solution)/shard_map/ppermute | solution.py:403
  31.8 1.0 %collective-permute-start.4 = (f32[2,32,128]{2,1,0:T(8,128)S(1)}, f32[2,32,128]{2,1,0:T(8,128)S(1)}, u32[]{:S(2)}, u32[]{:S(2)}) collective-permute-start(f32[2,32,128]{2,1,0:T(8,128)S(1)} %get-tuple-element.38), channel_id=1, source_target_pairs={{0,96},{32,64},{64,32},{96,0},{128,224},{160,192},{192,160},{224,1... | collective-permute-start | bytes 98312 | tf_op jit(solution)/shard_map/ppermute | solution.py:403
  32.8 2.4 %prepare.1 = (s32[4,264]{1,0:T(4,128)S(1)}, f32[3,264]{1,0:T(4,128)S(1)}, f32[3,64,128]{2,1,0:T(8,128)S(1)}) custom-call(s32[8,16]{1,0:T(8,128)S(1)} %get-tuple-element.23.levels, s32[2,8,16]{2,1,0:T(8,128)S(1)} %get-tuple-element.24.neighbours, f32[8]{0:T(128)S(1)} %get-tuple-element.25.decay, f32[2,8]{1,0:T(2,128)S(1)} %get-tuple-element.26.bath, ...), custom_call_target="tpu_custom_call" | custom-call | tf_op jit(solution)/shard_map/prepare/pallas_call | solution.py:418
  35.2 0.0 collective-permute-done.other
  35.2 0.5 sites.1
  35.7 0.0 collective-permute-done.2.refs_0_
  35.7 0.0 collective-permute-done.3.refs_1_
  35.7 0.7 collective-permute-done.4.refs_2_
  36.4 3.3 %rows.1 = f32[512,128]{1,0:T(8,128)S(1)} custom-call(s32[4,264]{1,0:T(4,128)S(1)} %get-tuple-element.28.ints_far, f32[3,264]{1,0:T(4,128)S(1)} %get-tuple-element.29.floats_far, f32[3,64,128]{2,1,0:T(8,128)S(1)} %get-tuple-element.30.fields, bf16[512,512]{1,0:T(8,128)(2,1)S(1)} %get-tuple-element.32.h_high, bf16[512,512]{1,0:T(8,128)(2,1)S(1)} %get-tuple-element.33.h_low, ...), custom_call_target="tpu_custom_call" | custom-call | tf_op jit(solution)/shard_map/rows/pallas_call | solution.py:442
  39.7 26.5 %all_to_all.16 = f32[256,2,128]{2,1,0:T(2,128)S(1)} all-to-all(f32[256,2,128]{2,1,0:T(2,128)S(1)} %bitcast.9), channel_id=1, replica_groups=mesh['hier'=8,'row'=32] {'row','hier'}, dimensions={0} | all-to-all | bytes 524288 | tf_op jit(solution)/shard_map/all_to_all | solution.py:458
  66.2 1.2 %columns.1 = (f32[256,128]{1,0:T(8,128)}, f32[512,128]{1,0:T(8,128)S(1)}) custom-call(f32[512,128]{1,0:T(8,128)S(1)} %bitcast.10, bf16[512,512]{1,0:T(8,128)(2,1)S(1)} %get-tuple-element.32.h_high, bf16[512,512]{1,0:T(8,128)(2,1)S(1)} %get-tuple-element.33.h_low), custom_call_target="tpu_custom_call" | custom-call | tf_op jit(solution)/shard_map/columns/pallas_call | solution.py:462
  67.4 0.0 copy-start
  67.4 4.4 %all-to-all-start.2 = ((f32[32,8,128]{2,1,0:T(8,128)}), f32[32,8,128]{2,1,0:T(8,128)S(1)}, u32[]{:S(2)}, u32[]{:S(2)}) async-start(f32[32,8,128]{2,1,0:T(8,128)} %bitcast.6), calls=%async_computation.2 | async-start | bytes 262144 | tf_op jit(solution)/shard_map/all_to_all | solution.py:471
  71.8 0.0 copy-done
  71.8 0.1 base.1
  71.9 7.7 %all-to-all-done.2 = f32[32,8,128]{2,1,0:T(8,128)S(1)} async-done(((f32[32,8,128]{2,1,0:T(8,128)}), f32[32,8,128]{2,1,0:T(8,128)S(1)}, u32[]{:S(2)}, u32[]{:S(2)}) %all-to-all-start.2) | async-done | bytes 131104 | tf_op jit(solution)/shard_map/all_to_all | solution.py:471
  79.6 0.9 %finish.1 = f32[64,512]{1,0:T(8,128)} custom-call(f32[64,512]{1,0:T(8,128)S(1)} %base.1, f32[256,128]{1,0:T(8,128)S(1)} %bitcast.11), custom_call_target="tpu_custom_call" | custom-call | tf_op jit(solution)/shard_map/finish/pallas_call | solution.py:479
  (1 shorter events, 0.0 us)
Async XLA Ops:
  17.3 17.9 %collective-permute-start = (f32[16,40,128]{2,1,0:T(8,128)S(1)}, f32[16,40,128]{2,1,0:T(8,128)S(1)}, u32[]{:S(2)}, u32[]{:S(2)}) collective-permute-start(f32[16,40,128]{2,1,0:T(8,128)S(1)} %all_to_all.15.mine), channel_id=1, source_target_pairs={{0,1},{1,0},{2,3},{3,2},{4,5},{5,4},{6,7},{7,6},{8,9},{9,8},{10,11... | collective-permute-start | bytes 983048 | tf_op jit(solution)/shard_map/ppermute | solution.py:400
  19.5 9.4 %collective-permute-start.1 = (f32[4,32,128]{2,1,0:T(8,128)S(1)}, f32[4,32,128]{2,1,0:T(8,128)S(1)}, u32[]{:S(2)}, u32[]{:S(2)}) collective-permute-start(f32[4,32,128]{2,1,0:T(8,128)S(1)} %get-tuple-element.35), channel_id=1, source_target_pairs={{0,128},{32,160},{64,192},{96,224},{128,0},{160,32},{192,64},{224,... | collective-permute-start | bytes 196616 | tf_op jit(solution)/shard_map/ppermute | solution.py:403
  28.9 6.7 %collective-permute-start.2 = (f32[2,32,128]{2,1,0:T(8,128)S(1)}, f32[2,32,128]{2,1,0:T(8,128)S(1)}, u32[]{:S(2)}, u32[]{:S(2)}) collective-permute-start(f32[2,32,128]{2,1,0:T(8,128)S(1)} %get-tuple-element.36), channel_id=1, source_target_pairs={{0,32},{32,0},{64,96},{96,64},{128,160},{160,128},{192,224},{224,1... | collective-permute-start | bytes 98312 | tf_op jit(solution)/shard_map/ppermute | solution.py:403
  29.8 5.9 %collective-permute-start.3 = (f32[2,32,128]{2,1,0:T(8,128)S(1)}, f32[2,32,128]{2,1,0:T(8,128)S(1)}, u32[]{:S(2)}, u32[]{:S(2)}) collective-permute-start(f32[2,32,128]{2,1,0:T(8,128)S(1)} %get-tuple-element.37), channel_id=1, source_target_pairs={{0,64},{32,96},{64,0},{96,32},{128,192},{160,224},{192,128},{224,1... | collective-permute-start | bytes 98312 | tf_op jit(solution)/shard_map/ppermute | solution.py:403
  31.8 4.6 %collective-permute-start.4 = (f32[2,32,128]{2,1,0:T(8,128)S(1)}, f32[2,32,128]{2,1,0:T(8,128)S(1)}, u32[]{:S(2)}, u32[]{:S(2)}) collective-permute-start(f32[2,32,128]{2,1,0:T(8,128)S(1)} %get-tuple-element.38), channel_id=1, source_target_pairs={{0,96},{32,64},{64,32},{96,0},{128,224},{160,192},{192,160},{224,1... | collective-permute-start | bytes 98312 | tf_op jit(solution)/shard_map/ppermute | solution.py:403
  67.4 4.4 %copy-start = (f32[2,2,16,512]{3,2,1,0:T(8,128)S(1)}, f32[2,2,16,512]{3,2,1,0:T(8,128)}, u32[]{:S(2)}) copy-start(f32[2,2,16,512]{3,2,1,0:T(8,128)} %param.7) | copy-start | bytes 393220
  67.4 12.2 %all-to-all-start.2 = ((f32[32,8,128]{2,1,0:T(8,128)}), f32[32,8,128]{2,1,0:T(8,128)S(1)}, u32[]{:S(2)}, u32[]{:S(2)}) async-start(f32[32,8,128]{2,1,0:T(8,128)} %bitcast.6), calls=%async_computation.2 | async-start | bytes 262144 | tf_op jit(solution)/shard_map/all_to_all | solution.py:471

commit v3 on v2

--- a/solution.py
+++ b/solution.py
@@ -176,31 +176,31 @@
             fields[2, here, :] = there
 
 
-def mix(ints, floats, fields, source, both, right):
+def mix(ints, floats, fields, *jobs):
     def step(e, carry):
         m = ints[0, e]
         q = ints[1, e]
         k = pl.multiple_of(ints[2, e], 8)
         even = floats[0, e]
         odd = floats[1, e]
-        xm, ym = source[m], source[m + 2]
-        xq, yq = source[q], source[q + 2]
-        if both is not None:
-            d = fields[0, pl.ds(k, 8), :]
-            f = odd * d
-            g = even * fields[1, pl.ds(k, 8), :]
+        d = fields[0, pl.ds(k, 8), :]
+        f = odd * d
+        g = even * fields[1, pl.ds(k, 8), :]
+        for source, both, right in jobs:
+            xm, ym = source[m], source[m + 2]
+            xq, yq = source[q], source[q + 2]
             both[m] = both[m] + (g * xq + f * yq)
             both[m + 2] = both[m + 2] + (g * yq - f * xq)
             both[q] = both[q] + d * ym
             both[q + 2] = both[q + 2] - d * xm
-        if right is not None:
-            c = fields[2, pl.ds(k, 8), :]
-            g = even * c
-            f = odd * c
-            right[m] = right[m] + (g * xq - f * yq)
-            right[m + 2] = right[m + 2] + (g * yq + f * xq)
-            right[q] = right[q] - c * ym
-            right[q + 2] = right[q + 2] + c * xm
+            if right is not None:
+                c = fields[2, pl.ds(k, 8), :]
+                gr = even * c
+                fr = odd * c
+                right[m] = right[m] + (gr * xq - fr * yq)
+                right[m + 2] = right[m + 2] + (gr * yq + fr * xq)
+                right[q] = right[q] - c * ym
+                right[q + 2] = right[q + 2] + c * xm
         return carry
 
     lax.fori_loop(0, ints[3, 0], step, 0)
@@ -310,22 +310,21 @@
     for fetch in fetches:
         fetch.wait()
     first[...] = decayed(floats, state)
-    mix(ints, floats, fields, state, first, right)
+    mix(ints, floats, fields, (state, first, right))
     first[...] = A2 * state[...] + A3 * first[...]
     second[...] = decayed(floats, first)
-    mix(ints, floats, fields, first, second, None)
     v1, edge = apply([first[...] + A3 * p_value, p_value + right[...]])
     damped = decayed(floats, p)
     ep[...] = damped
     bp[...] = damped + edge
-    mix(ints, floats, fields, p, ep, bp)
+    mix(ints, floats, fields, (p, ep, bp), (first, second, None))
     k_value = A2 * p_value + 3 * A3 * bp[...]
     z_value = 0.5 * A1 * s_value + v1 + A3 * ep[...] + 0.5 * second[...]
     v2 = z_value + 0.5 * A1 * s_value + 0.5 * second[...]
     (g_value,) = apply([v2])
     p[...] = z_value
     ep[...] = g_value + decayed(floats, p)
-    mix(ints, floats, fields, p, ep, None)
+    mix(ints, floats, fields, (p, ep, None))
     both = jnp.concatenate(
         [k_value.reshape(8, 4, 8, 128), ep[...].reshape(8, 4, 8, 128)], axis=1
     )

time: 80.8 us -> 80.5 us (level)
  no operation moved by 1% of the time
where the time goes in v3:
time: 80.5 us; the launch traced here: 80.2 us
  blocking collectives  41.9 us (52%)
  starting transfers between devices  17.4 us (22%)
  waiting for transfers between devices  10.8 us (13%)
  Pallas kernels  9.98 us (12%)
    all_to_all x1, blocking collectives, on_device(): lax.all_to_all(message.reshape(256, 2, 128), ('row', 'hier'), 0, 0, tiled...  26.5 us
    all_to_all x1, blocking collectives, on_device(): lax.all_to_all(copies, 'row', 0, 0, axis_index_groups=SAME_CORE, tiled=True)  15.4 us
    ppermute x4, starting transfers between devices, swap(): return lax.ppermute(block, 'hier', [(i, i ^ s) for i in range(PLANES)])  10.8 us
    all_to_all x1, waiting for transfers between devices, on_device(): lax.all_to_all(message.reshape(2 * CHIPS, 8, 128), 'row', 0, 0, tiled=True)  7.65 us
    all_to_all x1, starting transfers between devices, on_device(): lax.all_to_all(message.reshape(2 * CHIPS, 8, 128), 'row', 0, 0, tiled=True)  4.36 us
    ppermute x4, waiting for transfers between devices, swap(): return lax.ppermute(block, 'hier', [(i, i ^ s) for i in range(PLANES)])  3.18 us
    pallas_call x1, Pallas kernels, on_device(): pl.pallas_call(rows_kernel, out_shape=f32(512, 128), in_specs=[ANY] * 2 +...  3.01 us
    pallas_call x1, Pallas kernels, on_device(): pl.pallas_call(prepare_kernel, out_shape=[jax.ShapeDtypeStruct((4, EDGES)...  2.37 us
  transfers between devices with their start and end apart: 6, of which 3 were waited for; matrix products, arithmetic and copies ran while one was open for 0% of the time, Pallas kernels for 4%

profile of v3, /device:TPU:1, one launch (start us, length us, event | category | flops | bytes accessed | tf_op | source)
XLA Modules:
  0.0 80.2 jit_solution(7019532783398613656)
XLA Ops:
  0.0 1.8 %split.1 = (f32[16,40,128]{2,1,0:T(8,128)}, f32[4,32,128]{2,1,0:T(8,128)S(1)}, f32[4,32,128]{2,1,0:T(8,128)S(1)}, s32[8,16]{1,0:T(8,128)S(1)}, s32[2,8,16]{2,1,0...) custom-call(f32[4,16,512]{2,1,0:T(8,128)} %bitcast.12, f32[16,512]{1,0:T(8,128)} %hamiltonian.1, ...), custom_call_target="tpu_custom_call" | custom-call | tf_op jit(solution)/shard_map/split/pallas_call | solution.py:378
  1.8 15.4 %all_to_all.15.mine = f32[16,40,128]{2,1,0:T(8,128)S(1)} all-to-all(f32[16,40,128]{2,1,0:T(8,128)} %get-tuple-element.31), channel_id=1, replica_groups={{0,2,4,6,8,10,12,14,16,18,20,22,24,26,28,30},{1,3,5,7,9,11,13,15,17,19,..., dimensions={0} | all-to-all | bytes 655360 | tf_op jit(solution)/shard_map/all_to_all | solution.py:398
  17.3 2.3 %collective-permute-start = (f32[16,40,128]{2,1,0:T(8,128)S(1)}, f32[16,40,128]{2,1,0:T(8,128)S(1)}, u32[]{:S(2)}, u32[]{:S(2)}) collective-permute-start(f32[16,40,128]{2,1,0:T(8,128)S(1)} %all_to_all.15.mine), channel_id=1, source_target_pairs={{0,1},{1,0},{2,3},{3,2},{4,5},{5,4},{6,7},{7,6},{8,9},{9,8},{10,11... | collective-permute-start | bytes 983048 | tf_op jit(solution)/shard_map/ppermute | solution.py:399
  19.5 6.9 %collective-permute-start.1 = (f32[4,32,128]{2,1,0:T(8,128)S(1)}, f32[4,32,128]{2,1,0:T(8,128)S(1)}, u32[]{:S(2)}, u32[]{:S(2)}) collective-permute-start(f32[4,32,128]{2,1,0:T(8,128)S(1)} %get-tuple-element.35), channel_id=1, source_target_pairs={{0,128},{32,160},{64,192},{96,224},{128,0},{160,32},{192,64},{224,... | collective-permute-start | bytes 196616 | tf_op jit(solution)/shard_map/ppermute | solution.py:402
  26.5 2.5 %collective-permute-done.1.far_blocks = f32[4,32,128]{2,1,0:T(8,128)S(1)} collective-permute-done((f32[4,32,128]{2,1,0:T(8,128)S(1)}, f32[4,32,128]{2,1,0:T(8,128)S(1)}, u32[]{:S(2)}, u32[]{:S(2)}) %collective-permute-start.1) | collective-permute-done | bytes 65568 | tf_op jit(solution)/shard_map/ppermute | solution.py:402
  28.9 0.8 %collective-permute-start.2 = (f32[2,32,128]{2,1,0:T(8,128)S(1)}, f32[2,32,128]{2,1,0:T(8,128)S(1)}, u32[]{:S(2)}, u32[]{:S(2)}) collective-permute-start(f32[2,32,128]{2,1,0:T(8,128)S(1)} %get-tuple-element.36), channel_id=1, source_target_pairs={{0,32},{32,0},{64,96},{96,64},{128,160},{160,128},{192,224},{224,1... | collective-permute-start | bytes 98312 | tf_op jit(solution)/shard_map/ppermute | solution.py:402
  29.8 2.1 %collective-permute-start.3 = (f32[2,32,128]{2,1,0:T(8,128)S(1)}, f32[2,32,128]{2,1,0:T(8,128)S(1)}, u32[]{:S(2)}, u32[]{:S(2)}) collective-permute-start(f32[2,32,128]{2,1,0:T(8,128)S(1)} %get-tuple-element.37), channel_id=1, source_target_pairs={{0,64},{32,96},{64,0},{96,32},{128,192},{160,224},{192,128},{224,1... | collective-permute-start | bytes 98312 | tf_op jit(solution)/shard_map/ppermute | solution.py:402
  31.8 1.0 %collective-permute-start.4 = (f32[2,32,128]{2,1,0:T(8,128)S(1)}, f32[2,32,128]{2,1,0:T(8,128)S(1)}, u32[]{:S(2)}, u32[]{:S(2)}) collective-permute-start(f32[2,32,128]{2,1,0:T(8,128)S(1)} %get-tuple-element.38), channel_id=1, source_target_pairs={{0,96},{32,64},{64,32},{96,0},{128,224},{160,192},{192,160},{224,1... | collective-permute-start | bytes 98312 | tf_op jit(solution)/shard_map/ppermute | solution.py:402
  32.8 2.4 %prepare.1 = (s32[4,264]{1,0:T(4,128)S(1)}, f32[3,264]{1,0:T(4,128)S(1)}, f32[3,64,128]{2,1,0:T(8,128)S(1)}) custom-call(s32[8,16]{1,0:T(8,128)S(1)} %get-tuple-element.23.levels, s32[2,8,16]{2,1,0:T(8,128)S(1)} %get-tuple-element.24.neighbours, f32[8]{0:T(128)S(1)} %get-tuple-element.25.decay, f32[2,8]{1,0:T(2,128)S(1)} %get-tuple-element.26.bath, ...), custom_call_target="tpu_custom_call" | custom-call | tf_op jit(solution)/shard_map/prepare/pallas_call | solution.py:417
  35.2 0.0 collective-permute-done.other
  35.2 0.5 sites.1
  35.7 0.0 collective-permute-done.2.refs_0_
  35.7 0.0 collective-permute-done.3.refs_1_
  35.7 0.7 collective-permute-done.4.refs_2_
  36.4 3.0 %rows.1 = f32[512,128]{1,0:T(8,128)S(1)} custom-call(s32[4,264]{1,0:T(4,128)S(1)} %get-tuple-element.28.ints_far, f32[3,264]{1,0:T(4,128)S(1)} %get-tuple-element.29.floats_far, f32[3,64,128]{2,1,0:T(8,128)S(1)} %get-tuple-element.30.fields, bf16[512,512]{1,0:T(8,128)(2,1)S(1)} %get-tuple-element.32.h_high, bf16[512,512]{1,0:T(8,128)(2,1)S(1)} %get-tuple-element.33.h_low, ...), custom_call_target="tpu_custom_call" | custom-call | tf_op jit(solution)/shard_map/rows/pallas_call | solution.py:441
  39.4 26.5 %all_to_all.16 = f32[256,2,128]{2,1,0:T(2,128)S(1)} all-to-all(f32[256,2,128]{2,1,0:T(2,128)S(1)} %bitcast.9), channel_id=1, replica_groups=mesh['hier'=8,'row'=32] {'row','hier'}, dimensions={0} | all-to-all | bytes 524288 | tf_op jit(solution)/shard_map/all_to_all | solution.py:457
  65.9 1.2 %columns.1 = (f32[256,128]{1,0:T(8,128)}, f32[512,128]{1,0:T(8,128)S(1)}) custom-call(f32[512,128]{1,0:T(8,128)S(1)} %bitcast.10, bf16[512,512]{1,0:T(8,128)(2,1)S(1)} %get-tuple-element.32.h_high, bf16[512,512]{1,0:T(8,128)(2,1)S(1)} %get-tuple-element.33.h_low), custom_call_target="tpu_custom_call" | custom-call | tf_op jit(solution)/shard_map/columns/pallas_call | solution.py:461
  67.1 0.0 copy-start
  67.1 4.4 %all-to-all-start.2 = ((f32[32,8,128]{2,1,0:T(8,128)}), f32[32,8,128]{2,1,0:T(8,128)S(1)}, u32[]{:S(2)}, u32[]{:S(2)}) async-start(f32[32,8,128]{2,1,0:T(8,128)} %bitcast.6), calls=%async_computation.2 | async-start | bytes 262144 | tf_op jit(solution)/shard_map/all_to_all | solution.py:470
  71.5 0.0 copy-done
  71.5 0.1 base.1
  71.6 7.7 %all-to-all-done.2 = f32[32,8,128]{2,1,0:T(8,128)S(1)} async-done(((f32[32,8,128]{2,1,0:T(8,128)}), f32[32,8,128]{2,1,0:T(8,128)S(1)}, u32[]{:S(2)}, u32[]{:S(2)}) %all-to-all-start.2) | async-done | bytes 131104 | tf_op jit(solution)/shard_map/all_to_all | solution.py:470
  79.3 0.9 %finish.1 = f32[64,512]{1,0:T(8,128)} custom-call(f32[64,512]{1,0:T(8,128)S(1)} %base.1, f32[256,128]{1,0:T(8,128)S(1)} %bitcast.11), custom_call_target="tpu_custom_call" | custom-call | tf_op jit(solution)/shard_map/finish/pallas_call | solution.py:478
  (1 shorter events, 0.0 us)
Async XLA Ops:
  17.3 17.9 %collective-permute-start = (f32[16,40,128]{2,1,0:T(8,128)S(1)}, f32[16,40,128]{2,1,0:T(8,128)S(1)}, u32[]{:S(2)}, u32[]{:S(2)}) collective-permute-start(f32[16,40,128]{2,1,0:T(8,128)S(1)} %all_to_all.15.mine), channel_id=1, source_target_pairs={{0,1},{1,0},{2,3},{3,2},{4,5},{5,4},{6,7},{7,6},{8,9},{9,8},{10,11... | collective-permute-start | bytes 983048 | tf_op jit(solution)/shard_map/ppermute | solution.py:399
  19.5 9.4 %collective-permute-start.1 = (f32[4,32,128]{2,1,0:T(8,128)S(1)}, f32[4,32,128]{2,1,0:T(8,128)S(1)}, u32[]{:S(2)}, u32[]{:S(2)}) collective-permute-start(f32[4,32,128]{2,1,0:T(8,128)S(1)} %get-tuple-element.35), channel_id=1, source_target_pairs={{0,128},{32,160},{64,192},{96,224},{128,0},{160,32},{192,64},{224,... | collective-permute-start | bytes 196616 | tf_op jit(solution)/shard_map/ppermute | solution.py:402
  28.9 6.7 %collective-permute-start.2 = (f32[2,32,128]{2,1,0:T(8,128)S(1)}, f32[2,32,128]{2,1,0:T(8,128)S(1)}, u32[]{:S(2)}, u32[]{:S(2)}) collective-permute-start(f32[2,32,128]{2,1,0:T(8,128)S(1)} %get-tuple-element.36), channel_id=1, source_target_pairs={{0,32},{32,0},{64,96},{96,64},{128,160},{160,128},{192,224},{224,1... | collective-permute-start | bytes 98312 | tf_op jit(solution)/shard_map/ppermute | solution.py:402
  29.8 5.9 %collective-permute-start.3 = (f32[2,32,128]{2,1,0:T(8,128)S(1)}, f32[2,32,128]{2,1,0:T(8,128)S(1)}, u32[]{:S(2)}, u32[]{:S(2)}) collective-permute-start(f32[2,32,128]{2,1,0:T(8,128)S(1)} %get-tuple-element.37), channel_id=1, source_target_pairs={{0,64},{32,96},{64,0},{96,32},{128,192},{160,224},{192,128},{224,1... | collective-permute-start | bytes 98312 | tf_op jit(solution)/shard_map/ppermute | solution.py:402
  31.8 4.6 %collective-permute-start.4 = (f32[2,32,128]{2,1,0:T(8,128)S(1)}, f32[2,32,128]{2,1,0:T(8,128)S(1)}, u32[]{:S(2)}, u32[]{:S(2)}) collective-permute-start(f32[2,32,128]{2,1,0:T(8,128)S(1)} %get-tuple-element.38), channel_id=1, source_target_pairs={{0,96},{32,64},{64,32},{96,0},{128,224},{160,192},{192,160},{224,1... | collective-permute-start | bytes 98312 | tf_op jit(solution)/shard_map/ppermute | solution.py:402
  67.1 4.4 %copy-start = (f32[2,2,16,512]{3,2,1,0:T(8,128)S(1)}, f32[2,2,16,512]{3,2,1,0:T(8,128)}, u32[]{:S(2)}) copy-start(f32[2,2,16,512]{3,2,1,0:T(8,128)} %param.7) | copy-start | bytes 393220
  67.1 12.2 %all-to-all-start.2 = ((f32[32,8,128]{2,1,0:T(8,128)}), f32[32,8,128]{2,1,0:T(8,128)S(1)}, u32[]{:S(2)}, u32[]{:S(2)}) async-start(f32[32,8,128]{2,1,0:T(8,128)} %bitcast.6), calls=%async_computation.2 | async-start | bytes 262144 | tf_op jit(solution)/shard_map/all_to_all | solution.py:470

commit v4 on v3

--- a/solution.py
+++ b/solution.py
@@ -358,12 +358,9 @@
     message[...] = jnp.where(lane < 64, tiles[:, 0].reshape(256, 128), upper)
 
 
-def base_kernel(density, total, base):
-    base[...] = density[...] + jnp.transpose(total[...])[:64]
-
-
-def finish_kernel(base, received, out):
+def finish_kernel(density, total, received, out):
     value = swap_blocks(received[...].reshape(4, 8, 8, 128))
+    base = density[...] + jnp.transpose(total[...])[:64]
     for g in range(4):
         for half in range(2):
             for p in range(4):
@@ -471,18 +468,14 @@
         message.reshape(2 * CHIPS, 8, 128), "row", 0, 0, tiled=True
     ).reshape(256, 128)
 
-    base = pl.pallas_call(
-        base_kernel, out_shape=f32(64, 512), in_specs=[VMEM] * 2, out_specs=VMEM, name="base",
-        compiler_params=PARAMS,
-    )(density.reshape(64, 512), *near(total))
     out = pl.pallas_call(
         finish_kernel,
         out_shape=jax.ShapeDtypeStruct((64, 512), jnp.float32),
-        in_specs=[VMEM] * 2,
+        in_specs=[VMEM] * 3,
         out_specs=VMEM,
         name="finish",
         compiler_params=PARAMS,
-    )(*near(base, received))
+    )(*near(density.reshape(64, 512), total, received))
     return out.reshape(2, 2, 16, 512)
 
 

time: 80.5 us -> 79.2 us (0.984)
  blocking collectives: 41.9 us -> 53.4 us
  waiting for transfers between devices: 10.8 us -> 3.19 us
  starting transfers between devices: 17.4 us -> 13 us
    all_to_all x0 -> x1, blocking collectives: none -> 11.5 us  [on_device(): lax.all_to_all(message.reshape(2 * CHIPS, 8, 128), 'row', 0, 0, tiled=True)]
    all_to_all x1 -> x0, waiting for transfers between devices: 7.65 us -> none  [on_device(): lax.all_to_all(message.reshape(2 * CHIPS, 8, 128), 'row', 0, 0, tiled=True)]
    all_to_all x1 -> x0, starting transfers between devices: 4.36 us -> none  [on_device(): lax.all_to_all(message.reshape(2 * CHIPS, 8, 128), 'row', 0, 0, tiled=True)]
  transfers between devices with their start and end apart: 6 -> 5, of which waited for: 3 -> 2; matrix products, arithmetic and copies ran while one was open for 0% -> 0% of each run, Pallas kernels for 4% -> 4%
where the time goes in v4:
time: 79.2 us; the launch traced here: 79 us
  blocking collectives  53.4 us (67%)
  starting transfers between devices  13 us (16%)
  Pallas kernels  9.29 us (12%)
  waiting for transfers between devices  3.19 us (4%)
    all_to_all x1, blocking collectives, on_device(): lax.all_to_all(message.reshape(256, 2, 128), ('row', 'hier'), 0, 0, tiled...  26.5 us
    all_to_all x1, blocking collectives, on_device(): lax.all_to_all(copies, 'row', 0, 0, axis_index_groups=SAME_CORE, tiled=True)  15.4 us
    all_to_all x1, blocking collectives, on_device(): lax.all_to_all(message.reshape(2 * CHIPS, 8, 128), 'row', 0, 0, tiled=True)  11.5 us
    ppermute x4, starting transfers between devices, swap(): return lax.ppermute(block, 'hier', [(i, i ^ s) for i in range(PLANES)])  10.8 us
    ppermute x4, waiting for transfers between devices, swap(): return lax.ppermute(block, 'hier', [(i, i ^ s) for i in range(PLANES)])  3.18 us
    pallas_call x1, Pallas kernels, on_device(): pl.pallas_call(rows_kernel, out_shape=f32(512, 128), in_specs=[ANY] * 2 +...  3.01 us
    pallas_call x1, Pallas kernels, on_device(): pl.pallas_call(prepare_kernel, out_shape=[jax.ShapeDtypeStruct((4, EDGES)...  2.37 us
    ppermute x1, starting transfers between devices, on_device(): other = lax.ppermute(mine, 'row', [(i, i ^ 1) for i in range(2 * CHIPS)])  2.27 us
  transfers between devices with their start and end apart: 5, of which 2 were waited for; matrix products, arithmetic and copies ran while one was open for 0% of the time, Pallas kernels for 4%

profile of v4, /device:TPU:1, one launch (start us, length us, event | category | flops | bytes accessed | tf_op | source)
XLA Modules:
  0.0 79.0 jit_solution(8714711962988272465)
XLA Ops:
  0.0 1.8 %split.1 = (f32[16,40,128]{2,1,0:T(8,128)}, f32[4,32,128]{2,1,0:T(8,128)S(1)}, f32[4,32,128]{2,1,0:T(8,128)S(1)}, s32[8,16]{1,0:T(8,128)S(1)}, s32[2,8,16]{2,1,0...) custom-call(f32[4,16,512]{2,1,0:T(8,128)} %bitcast.11, f32[16,512]{1,0:T(8,128)} %hamiltonian.1, ...), custom_call_target="tpu_custom_call" | custom-call | tf_op jit(solution)/shard_map/split/pallas_call | solution.py:375
  1.8 15.4 %all_to_all.15.mine = f32[16,40,128]{2,1,0:T(8,128)S(1)} all-to-all(f32[16,40,128]{2,1,0:T(8,128)} %get-tuple-element.31), channel_id=1, replica_groups={{0,2,4,6,8,10,12,14,16,18,20,22,24,26,28,30},{1,3,5,7,9,11,13,15,17,19,..., dimensions={0} | all-to-all | bytes 655360 | tf_op jit(solution)/shard_map/all_to_all | solution.py:395
  17.3 2.3 %collective-permute-start = (f32[16,40,128]{2,1,0:T(8,128)S(1)}, f32[16,40,128]{2,1,0:T(8,128)S(1)}, u32[]{:S(2)}, u32[]{:S(2)}) collective-permute-start(f32[16,40,128]{2,1,0:T(8,128)S(1)} %all_to_all.15.mine), channel_id=1, source_target_pairs={{0,1},{1,0},{2,3},{3,2},{4,5},{5,4},{6,7},{7,6},{8,9},{9,8},{10,11... | collective-permute-start | bytes 983048 | tf_op jit(solution)/shard_map/ppermute | solution.py:396
  19.6 6.9 %collective-permute-start.1 = (f32[4,32,128]{2,1,0:T(8,128)S(1)}, f32[4,32,128]{2,1,0:T(8,128)S(1)}, u32[]{:S(2)}, u32[]{:S(2)}) collective-permute-start(f32[4,32,128]{2,1,0:T(8,128)S(1)} %get-tuple-element.35), channel_id=1, source_target_pairs={{0,128},{32,160},{64,192},{96,224},{128,0},{160,32},{192,64},{224,... | collective-permute-start | bytes 196616 | tf_op jit(solution)/shard_map/ppermute | solution.py:399
  26.5 2.5 %collective-permute-done.1.far_blocks = f32[4,32,128]{2,1,0:T(8,128)S(1)} collective-permute-done((f32[4,32,128]{2,1,0:T(8,128)S(1)}, f32[4,32,128]{2,1,0:T(8,128)S(1)}, u32[]{:S(2)}, u32[]{:S(2)}) %collective-permute-start.1) | collective-permute-done | bytes 65568 | tf_op jit(solution)/shard_map/ppermute | solution.py:399
  28.9 0.8 %collective-permute-start.2 = (f32[2,32,128]{2,1,0:T(8,128)S(1)}, f32[2,32,128]{2,1,0:T(8,128)S(1)}, u32[]{:S(2)}, u32[]{:S(2)}) collective-permute-start(f32[2,32,128]{2,1,0:T(8,128)S(1)} %get-tuple-element.36), channel_id=1, source_target_pairs={{0,32},{32,0},{64,96},{96,64},{128,160},{160,128},{192,224},{224,1... | collective-permute-start | bytes 98312 | tf_op jit(solution)/shard_map/ppermute | solution.py:399
  29.8 2.1 %collective-permute-start.3 = (f32[2,32,128]{2,1,0:T(8,128)S(1)}, f32[2,32,128]{2,1,0:T(8,128)S(1)}, u32[]{:S(2)}, u32[]{:S(2)}) collective-permute-start(f32[2,32,128]{2,1,0:T(8,128)S(1)} %get-tuple-element.37), channel_id=1, source_target_pairs={{0,64},{32,96},{64,0},{96,32},{128,192},{160,224},{192,128},{224,1... | collective-permute-start | bytes 98312 | tf_op jit(solution)/shard_map/ppermute | solution.py:399
  31.8 1.0 %collective-permute-start.4 = (f32[2,32,128]{2,1,0:T(8,128)S(1)}, f32[2,32,128]{2,1,0:T(8,128)S(1)}, u32[]{:S(2)}, u32[]{:S(2)}) collective-permute-start(f32[2,32,128]{2,1,0:T(8,128)S(1)} %get-tuple-element.38), channel_id=1, source_target_pairs={{0,96},{32,64},{64,32},{96,0},{128,224},{160,192},{192,160},{224,1... | collective-permute-start | bytes 98312 | tf_op jit(solution)/shard_map/ppermute | solution.py:399
  32.8 2.4 %prepare.1 = (s32[4,264]{1,0:T(4,128)S(1)}, f32[3,264]{1,0:T(4,128)S(1)}, f32[3,64,128]{2,1,0:T(8,128)S(1)}) custom-call(s32[8,16]{1,0:T(8,128)S(1)} %get-tuple-element.23.levels, s32[2,8,16]{2,1,0:T(8,128)S(1)} %get-tuple-element.24.neighbours, f32[8]{0:T(128)S(1)} %get-tuple-element.25.decay, f32[2,8]{1,0:T(2,128)S(1)} %get-tuple-element.26.bath, ...), custom_call_target="tpu_custom_call" | custom-call | tf_op jit(solution)/shard_map/prepare/pallas_call | solution.py:414
  35.2 0.0 collective-permute-done.other
  35.2 0.5 sites.1
  35.7 0.0 collective-permute-done.2.refs_0_
  35.7 0.0 collective-permute-done.3.refs_1_
  35.7 0.7 collective-permute-done.4.refs_2_
  36.4 3.0 %rows.1 = f32[512,128]{1,0:T(8,128)S(1)} custom-call(s32[4,264]{1,0:T(4,128)S(1)} %get-tuple-element.28.ints_far, f32[3,264]{1,0:T(4,128)S(1)} %get-tuple-element.29.floats_far, f32[3,64,128]{2,1,0:T(8,128)S(1)} %get-tuple-element.30.fields, bf16[512,512]{1,0:T(8,128)(2,1)S(1)} %get-tuple-element.32.h_high, bf16[512,512]{1,0:T(8,128)(2,1)S(1)} %get-tuple-element.33.h_low, ...), custom_call_target="tpu_custom_call" | custom-call | tf_op jit(solution)/shard_map/rows/pallas_call | solution.py:438
  39.4 26.5 %all_to_all.16 = f32[256,2,128]{2,1,0:T(2,128)S(1)} all-to-all(f32[256,2,128]{2,1,0:T(2,128)S(1)} %bitcast.9), channel_id=1, replica_groups=mesh['hier'=8,'row'=32] {'row','hier'}, dimensions={0} | all-to-all | bytes 524288 | tf_op jit(solution)/shard_map/all_to_all | solution.py:454
  65.9 0.6 columns.1
  66.5 0.0 copy-start
  66.5 11.5 %all_to_all.17 = f32[32,8,128]{2,1,0:T(8,128)S(1)} all-to-all(f32[32,8,128]{2,1,0:T(8,128)S(1)} %bitcast.14), channel_id=1, replica_groups=mesh['hier'=8,'row'=32] {'row'}, dimensions={0} | all-to-all | bytes 262144 | tf_op jit(solution)/shard_map/all_to_all | solution.py:467
  78.0 0.0 copy-done
  78.0 1.0 %finish.1 = f32[64,512]{1,0:T(8,128)} custom-call(f32[64,512]{1,0:T(8,128)S(1)} %bitcast.12, f32[512,128]{1,0:T(8,128)S(1)} %get-tuple-element.39.total, f32[256,128]{1,0:T(8,128)S(1)} %bitcast.13), custom_call_target="tpu_custom_call" | custom-call | tf_op jit(solution)/shard_map/finish/pallas_call | solution.py:471
  (1 shorter events, 0.0 us)
Async XLA Ops:
  17.3 17.9 %collective-permute-start = (f32[16,40,128]{2,1,0:T(8,128)S(1)}, f32[16,40,128]{2,1,0:T(8,128)S(1)}, u32[]{:S(2)}, u32[]{:S(2)}) collective-permute-start(f32[16,40,128]{2,1,0:T(8,128)S(1)} %all_to_all.15.mine), channel_id=1, source_target_pairs={{0,1},{1,0},{2,3},{3,2},{4,5},{5,4},{6,7},{7,6},{8,9},{9,8},{10,11... | collective-permute-start | bytes 983048 | tf_op jit(solution)/shard_map/ppermute | solution.py:396
  19.6 9.4 %collective-permute-start.1 = (f32[4,32,128]{2,1,0:T(8,128)S(1)}, f32[4,32,128]{2,1,0:T(8,128)S(1)}, u32[]{:S(2)}, u32[]{:S(2)}) collective-permute-start(f32[4,32,128]{2,1,0:T(8,128)S(1)} %get-tuple-element.35), channel_id=1, source_target_pairs={{0,128},{32,160},{64,192},{96,224},{128,0},{160,32},{192,64},{224,... | collective-permute-start | bytes 196616 | tf_op jit(solution)/shard_map/ppermute | solution.py:399
  28.9 6.7 %collective-permute-start.2 = (f32[2,32,128]{2,1,0:T(8,128)S(1)}, f32[2,32,128]{2,1,0:T(8,128)S(1)}, u32[]{:S(2)}, u32[]{:S(2)}) collective-permute-start(f32[2,32,128]{2,1,0:T(8,128)S(1)} %get-tuple-element.36), channel_id=1, source_target_pairs={{0,32},{32,0},{64,96},{96,64},{128,160},{160,128},{192,224},{224,1... | collective-permute-start | bytes 98312 | tf_op jit(solution)/shard_map/ppermute | solution.py:399
  29.8 5.9 %collective-permute-start.3 = (f32[2,32,128]{2,1,0:T(8,128)S(1)}, f32[2,32,128]{2,1,0:T(8,128)S(1)}, u32[]{:S(2)}, u32[]{:S(2)}) collective-permute-start(f32[2,32,128]{2,1,0:T(8,128)S(1)} %get-tuple-element.37), channel_id=1, source_target_pairs={{0,64},{32,96},{64,0},{96,32},{128,192},{160,224},{192,128},{224,1... | collective-permute-start | bytes 98312 | tf_op jit(solution)/shard_map/ppermute | solution.py:399
  31.8 4.6 %collective-permute-start.4 = (f32[2,32,128]{2,1,0:T(8,128)S(1)}, f32[2,32,128]{2,1,0:T(8,128)S(1)}, u32[]{:S(2)}, u32[]{:S(2)}) collective-permute-start(f32[2,32,128]{2,1,0:T(8,128)S(1)} %get-tuple-element.38), channel_id=1, source_target_pairs={{0,96},{32,64},{64,32},{96,0},{128,224},{160,192},{192,160},{224,1... | collective-permute-start | bytes 98312 | tf_op jit(solution)/shard_map/ppermute | solution.py:399
  66.5 11.5 %copy-start = (f32[2,2,16,512]{3,2,1,0:T(8,128)S(1)}, f32[2,2,16,512]{3,2,1,0:T(8,128)}, u32[]{:S(2)}) copy-start(f32[2,2,16,512]{3,2,1,0:T(8,128)} %param.7) | copy-start | bytes 393220
